TPU v7x, 32 devices: a whole 2x2x4 slice. The times are simulated.
32 devices in a mesh: dp: 8 (over z, x), tile: 4 (over y, core).
Axes of the slice: x: 2, y: 2, z: 4, core: 2. Of those that a mesh axis runs over, the one named last changes fastest.
Arguments:
- frames: bfloat16 [32, 4, 64, 256], P('dp', 'tile'), may hold values from -6 to 6
- kernels: bfloat16 [32, 9, 256, 256], P('dp'), may hold values from -0.125 to 0.125
- experts: int32 [32, 4, 4], P('dp', 'tile'), may hold values from 0 to 31, as said below
- counts: int32 [32, 4], P('dp', 'tile'), may hold values from 2 to 4
- gate_weights: float32 [32, 4, 4], P('dp', 'tile'), may hold values from 0.25 to 1
- cotangent: bfloat16 [32, 4, 64, 256], P('dp', 'tile'), may hold values from -6 to 6
Outputs:
- frames_out: bfloat16 [32, 4, 64, 256], P('dp', 'tile')
- input_grad: bfloat16 [32, 4, 64, 256], P('dp', 'tile')
- gate_grad: float32 [32, 4, 4], P('dp', 'tile')
- kernel_grad: float32 [32, 9, 256, 256], P('dp', None, None, 'tile')
Inputs may be any that keep to these rules, and one draw needn't show every extreme that they name: A tile's 4 experts have distinct values of id // 4. Among the 4 tiles of one device (frames d * 4 to (d + 1) * 4 - 1 at one tile index), each value of id // 4 is named by at most 2 tiles, by exactly 2 for some, and all its slots there name the same id. A tile uses its first counts slots; later slots are ignored.
All inputs are finite; a program needn't handle non-finite values.
Results may differ from a plain program's by a relative error of at most 0.005.
Values may be sent and summed in bfloat16 or wider, within the bound.
A program may use at most 256 MiB of HBM per device.

v0:
```python
import functools

import jax
import jax.numpy as jnp
from jax import lax
from jax.experimental import pallas as pl
from jax.experimental.pallas import tpu as pltpu
from jax.sharding import PartitionSpec as P

CAP = 2


def shifts(columns, rows):
    place = lax.broadcasted_iota(jnp.int32, (rows, 1), 0) % columns

    def later(v):
        return jnp.where(place == 0, 0.0, pltpu.roll(v, 1, 0))

    def sooner(v):
        return jnp.where(place == columns - 1, 0.0, pltpu.roll(v, rows - 1, 0))

    return later, sooner


def owner_kernel(
    pick_ref, weight_ref, place_ref, rim_ref,
    rows_ref, above_ref, below_ref, bank_ref, back_ref, edge_ref, gate_ref, out_ref, grad_ref,
):
    s = pl.program_id(0)
    cap = CAP
    columns, channels = back_ref.shape[3:]
    steps = out_ref.shape[1]
    rows = cap * columns
    later, sooner = shifts(columns, rows)

    @pl.when(s == 0)
    def _():
        @pl.loop(0, steps)
        def _(i):
            grad_ref[:, i] = jnp.zeros_like(grad_ref[:, i])

    back_ref[...] = jnp.zeros_like(back_ref)

    item = lax.broadcasted_iota(jnp.int32, (rows, 1), 0) // columns
    weight = jnp.zeros((rows, 1), jnp.float32)
    for c in range(cap):
        weight = jnp.where(item == c, weight_ref[s, c], weight)

    def gather(ref, *lead):
        return jnp.concatenate([ref[(0,) + lead + (place_ref[s, c],)] for c in range(cap)], axis=0)

    blank = jnp.zeros((rows, channels), jnp.bfloat16)
    window = [
        jnp.where(rim_ref[0] > 0, gather(above_ref), blank),
        gather(rows_ref, 0),
        jnp.where(rim_ref[1] > 0, gather(below_ref), blank),
    ]
    upstream = gather(rows_ref, 1).astype(jnp.float32)

    def column_term(db):
        total = jnp.dot(window[0], bank_ref[0, db], preferred_element_type=jnp.float32)
        for da in (1, 2):
            total = total + jnp.dot(
                window[da], bank_ref[0, 3 * da + db], preferred_element_type=jnp.float32
            )
        return total

    pre = column_term(1) + later(column_term(0)) + sooner(column_term(2))
    pre = pre.astype(jnp.bfloat16).astype(jnp.float32)
    squash = jax.nn.sigmoid(pre)
    activated = pre * squash
    slope = squash * (1.0 + pre * (1.0 - squash))

    def put(r, value):
        value = value.astype(jnp.bfloat16).reshape(cap, columns, channels)
        for c in reversed(range(cap)):
            back_ref[0, r, place_ref[s, c]] = value[c]

    put(1, weight * activated)
    gates = jnp.sum((upstream * activated).reshape(cap, columns, channels), axis=1)
    gates = jnp.broadcast_to(jnp.sum(gates, axis=1, keepdims=True), (cap, 128))
    gate_ref[0] = jnp.concatenate([gates, jnp.zeros((8 - cap, 128), jnp.float32)], axis=0)

    grad = (upstream * weight * slope).astype(jnp.bfloat16)
    for da in range(3):
        parts = [
            lax.dot_general(
                grad,
                bank_ref[0, 3 * da + db],
                (((1,), (1,)), ((), ())),
                preferred_element_type=jnp.float32,
            )
            for db in range(3)
        ]
        total = parts[1] + sooner(parts[0]) + later(parts[2])
        if da == 1:
            put(0, total)
        else:
            edge_ref[0, da // 2] = total.astype(jnp.bfloat16).reshape(cap, columns, channels)

    grad_wide = grad.astype(jnp.float32)
    moved = [sooner(grad_wide).astype(jnp.bfloat16), grad, later(grad_wide).astype(jnp.bfloat16)]
    e = pick_ref[s]
    chunks, _, share, _ = grad_ref.shape
    taps = bank_ref.shape[1]
    for db in range(3):
        for da in range(3):
            term = lax.dot_general(
                moved[db], window[da], (((0,), (0,)), ((), ())), preferred_element_type=jnp.float32
            )
            grad_ref[:, e * taps + 3 * da + db] += term.reshape(chunks, share, channels)

    @pl.when(s == pl.num_programs(0) - 1)
    def _():
        @pl.loop(0, steps)
        def _(i):
            out_ref[:, i] = grad_ref[:, i].astype(out_ref.dtype)


def owner(pick, weight, place, rim, rows, above, below, kernels, chunks):
    sources, _, frames, columns, channels = rows.shape
    experts, taps, _, outputs = kernels.shape
    spec = pltpu.PrefetchScalarGridSpec(
        num_scalar_prefetch=4,
        grid=(sources,),
        in_specs=[
            pl.BlockSpec((1, 2, frames, columns, channels), lambda s, *_: (s, 0, 0, 0, 0)),
            pl.BlockSpec((1, frames, columns, channels), lambda s, *_: (s, 0, 0, 0)),
            pl.BlockSpec((1, frames, columns, channels), lambda s, *_: (s, 0, 0, 0)),
            pl.BlockSpec((1, taps, channels, outputs), lambda s, p, *_: (p[s], 0, 0, 0)),
        ],
        out_specs=[
            pl.BlockSpec((1, 2, frames, columns, channels), lambda s, *_: (s, 0, 0, 0, 0)),
            pl.BlockSpec((1, 2, CAP, columns, channels), lambda s, *_: (s, 0, 0, 0, 0)),
            pl.BlockSpec((1, 8, 128), lambda s, *_: (s, 0, 0)),
            pl.BlockSpec(
                (chunks, experts * taps, outputs // chunks, channels),
                lambda s, *_: (0, 0, 0, 0),
                pipeline_mode=pl.Buffered(1),
            ),
        ],
        scratch_shapes=[
            pltpu.VMEM((chunks, experts * taps, outputs // chunks, channels), jnp.float32)
        ],
    )
    return pl.pallas_call(
        owner_kernel,
        grid_spec=spec,
        out_shape=[
            jax.ShapeDtypeStruct((sources, 2, frames, columns, channels), jnp.bfloat16),
            jax.ShapeDtypeStruct((sources, 2, CAP, columns, channels), jnp.bfloat16),
            jax.ShapeDtypeStruct((sources, 8, 128), jnp.float32),
            jax.ShapeDtypeStruct(
                (chunks, experts * taps, outputs // chunks, channels), jnp.bfloat16
            ),
        ],
        compiler_params=pltpu.CompilerParams(vmem_limit_bytes=48 * 1024 * 1024),
        name="owner",
    )(pick, weight, place, rim, rows, above, below, kernels)


def grid_of(owners):
    across = 1
    while across * across * 4 <= owners:
        across *= 2
    while owners % across:
        across -= 1
    return owners // across, across


def remote(src, dst, send, recv, dp, tile):
    return pltpu.make_async_remote_copy(
        src_ref=src,
        dst_ref=dst,
        send_sem=send,
        recv_sem=recv,
        device_id=(dp, tile),
        device_id_type=pl.DeviceIdType.MESH,
    )


def spread_kernel(
    deep, across, tiles,
    own_ref, note_ref, rows_ref, above_ref, below_ref, noted_ref,
    local_sem, main_recv, above_recv, below_recv, note_recv,
    up_send, down_send, side_send, above_send, below_send, note_send,
):
    me, t = lax.axis_index("dp"), lax.axis_index("tile")
    z, x = me // across, me % across
    owners = deep * across
    has_above, has_below = t > 0, t < tiles - 1

    barrier = pltpu.get_barrier_semaphore()

    def greet(dp, tile):
        pl.semaphore_signal(
            barrier, inc=1, device_id=(dp, tile), device_id_type=pl.DeviceIdType.MESH
        )

    for j in range(1, owners):
        greet((me + j) % owners, t)
    pl.when(has_above)(lambda: greet(me, t - 1))
    pl.when(has_below)(lambda: greet(me, t + 1))
    pl.semaphore_wait(
        barrier, owners - 1 + has_above.astype(jnp.int32) + has_below.astype(jnp.int32)
    )

    started = []

    def launch(cond, make):
        if cond is None:
            make().start()
        else:
            pl.when(cond)(lambda: make().start())
        started.append((cond, make))

    def both(a, b):
        if a is None:
            return b
        return a if b is None else jnp.logical_and(a, b)

    def halos(cond, s, block):
        launch(
            both(cond, has_below),
            lambda: remote(block, above_ref.at[s], above_send.at[s], above_recv.at[s], me, t + 1),
        )
        launch(
            both(cond, has_above),
            lambda: remote(block, below_ref.at[s], below_send.at[s], below_recv.at[s], me, t - 1),
        )

    def lift(cond, s, part, block):
        launch(
            both(cond, z < deep - 1),
            lambda: remote(
                block, rows_ref.at[s, part], up_send.at[part, s], main_recv.at[part, s],
                me + across, t,
            ),
        )

    def sink(cond, s, part, block):
        launch(
            both(cond, z > 0),
            lambda: remote(
                block, rows_ref.at[s, part], down_send.at[part, s], main_recv.at[part, s],
                me - across, t,
            ),
        )

    def side(cond, s, part, block):
        for j in range(1, across):
            launch(
                cond,
                lambda j=j: remote(
                    block,
                    rows_ref.at[s, part],
                    side_send.at[j - 1, part, s],
                    main_recv.at[part, s],
                    z * across + (x + j) % across,
                    t,
                ),
            )

    def arrive(cond, s, part):
        def wait():
            remote(
                rows_ref.at[s, part], rows_ref.at[s, part], up_send.at[part, s],
                main_recv.at[part, s], me, t,
            ).wait_recv()

        pl.when(cond)(wait) if cond is not None else wait()

    for j in range(1, owners):
        peer = (me + j) % owners
        launch(
            None,
            lambda j=j, peer=peer: remote(
                note_ref.at[peer], noted_ref.at[me], note_send.at[j - 1], note_recv.at[me], peer, t
            ),
        )
    for part in range(2):
        lift(None, me, part, own_ref.at[part])
        sink(None, me, part, own_ref.at[part])
        side(None, me, part, own_ref.at[part])
        if part == 0:
            halos(None, me, own_ref.at[0])
    kept = pltpu.make_async_copy(own_ref, rows_ref.at[me], local_sem.at[0])
    kept.start()
    noted = pltpu.make_async_copy(note_ref.at[me], noted_ref.at[me], local_sem.at[1])
    noted.start()

    def side_arrivals(k, part):
        for sign in (1, -1) if k else (1,):
            zs = z - sign * k
            cond = (zs >= 0 if sign > 0 else zs < deep) if k else None
            for j in range(1, across):
                s = zs * across + (x + j) % across
                arrive(cond, s, part)
                if part == 0:
                    halos(cond, s, rows_ref.at[s, 0])

    for k in range(1, deep):
        lower, upper = z - k, z + k
        for part in range(2):
            for zs, cond, onward in ((lower, lower >= 0, lift), (upper, upper < deep, sink)):
                s = zs * across + x
                arrive(cond, s, part)
                onward(cond, s, part, rows_ref.at[s, part])
                side(cond, s, part, rows_ref.at[s, part])
                if part == 0:
                    halos(cond, s, rows_ref.at[s, 0])
            side_arrivals(k - 1, part)
    for part in range(2):
        side_arrivals(deep - 1, part)

    for j in range(1, owners):
        s = (me + j) % owners
        remote(
            note_ref.at[s], noted_ref.at[s], note_send.at[j - 1], note_recv.at[s], s, t
        ).wait_recv()
    for s in range(owners):
        pl.when(has_above)(
            lambda s=s: remote(
                above_ref.at[s], above_ref.at[s], above_send.at[s], above_recv.at[s], me, t
            ).wait_recv()
        )
        pl.when(has_below)(
            lambda s=s: remote(
                below_ref.at[s], below_ref.at[s], below_send.at[s], below_recv.at[s], me, t
            ).wait_recv()
        )
    for cond, make in started:
        if cond is None:
            make().wait_send()
        else:
            pl.when(cond)(lambda make=make: make().wait_send())
    kept.wait()
    noted.wait()


def spread(own, note, owners, tiles):
    deep, across = grid_of(owners)
    dma = pltpu.SemaphoreType.DMA
    anywhere = pl.BlockSpec(memory_space=pl.ANY)
    return pl.pallas_call(
        functools.partial(spread_kernel, deep, across, tiles),
        out_shape=[
            jax.ShapeDtypeStruct((owners,) + own.shape, own.dtype),
            jax.ShapeDtypeStruct((owners,) + own.shape[1:], own.dtype),
            jax.ShapeDtypeStruct((owners,) + own.shape[1:], own.dtype),
            jax.ShapeDtypeStruct(note.shape, note.dtype),
        ],
        in_specs=[pl.BlockSpec(memory_space=pltpu.VMEM)] * 2,
        out_specs=[anywhere] * 4,
        scratch_shapes=[
            dma((2,)), dma((2, owners)), dma((owners,)), dma((owners,)), dma((owners,)),
            dma((2, owners)), dma((2, owners)), dma((max(across - 1, 1), 2, owners)),
            dma((owners,)), dma((owners,)), dma((owners,)),
        ],
        compiler_params=pltpu.CompilerParams(
            collective_id=0, has_side_effects=True, vmem_limit_bytes=8 * 1024 * 1024
        ),
        name="spread",
    )(own, note)


def collect_kernel(
    deep, across, high, cores,
    terms_ref, edge_ref, note_ref, gate_ref, bank_ref, own_ref,
    result_ref, input_ref, gated_ref, grad_ref,
    above, below, above_note, below_note, side_out, side_in, far_out, far_in, total, mate_in, band_out, band_in,
    local_sem, above_send, above_recv, below_send, below_recv,
    side_send, side_recv, far_send, far_recv, mate_send, mate_recv, band_send, band_recv,
    gate_send, gate_recv, tell_send, tell_recv,
):
    me, t = lax.axis_index("dp"), lax.axis_index("tile")
    z, x = me // across, me % across
    y, core = t // cores, t % cores
    owners, tiles = deep * across, high * cores
    frames = own_ref.shape[1]
    steps = grad_ref.shape[0]
    has_above, has_below = t > 0, t < tiles - 1

    barrier = pltpu.get_barrier_semaphore()
    for j in range(1, owners):
        pl.semaphore_signal(
            barrier, device_id=((me + j) % owners, t), device_id_type=pl.DeviceIdType.MESH
        )
    for j in range(1, tiles):
        pl.semaphore_signal(
            barrier, device_id=(me, (t + j) % tiles), device_id_type=pl.DeviceIdType.MESH
        )
    pl.semaphore_wait(barrier, owners - 1 + tiles - 1)

    started = []

    def launch(make, cond=None):
        if cond is None:
            make().start()
        else:
            pl.when(cond)(lambda: make().start())
        started.append((cond, make))

    ring = [(z + k) % deep for k in list(range(1, deep)) + [0]]

    def lower(s):
        return remote(edge_ref.at[s, 1], above.at[s], above_send.at[s], above_recv.at[s], me, t + 1)

    def upper(s):
        return remote(edge_ref.at[s, 0], below.at[s], below_send.at[s], below_recv.at[s], me, t - 1)

    def tell_lower():
        return remote(note_ref, above_note, tell_send.at[0], tell_recv.at[0], me, t + 1)

    def tell_upper():
        return remote(note_ref, below_note, tell_send.at[1], tell_recv.at[1], me, t - 1)

    launch(tell_lower, has_below)
    launch(tell_upper, has_above)
    for j in list(range(1, across)) + [0]:
        for zs in ring:
            s = zs * across + (x + j) % across
            launch(lambda s=s: lower(s), has_below)
            launch(lambda s=s: upper(s), has_above)

    bands = [(y + k) % high for k in list(range(1, high)) + [0]]
    pieces = mate_send.shape[2]
    length = steps // pieces
    for k, ys in enumerate(bands):
        for p in range(pieces):
            for j in range(1, cores):
                mate = (core + j) % cores
                launch(
                    lambda k=k, p=p, j=j, ys=ys, mate=mate: remote(
                        bank_ref.at[ys * cores + mate, pl.ds(p * length, length)],
                        mate_in.at[k, j - 1, pl.ds(p * length, length)],
                        mate_send.at[k, j - 1, p],
                        mate_recv.at[k, j - 1, p],
                        me,
                        y * cores + mate,
                    )
                )
    for j in range(1, owners):
        peer = (me + j) % owners
        launch(
            lambda j=j, peer=peer: remote(
                gate_ref.at[peer], gated_ref.at[me], gate_send.at[j - 1], gate_recv.at[j - 1], peer, t
            )
        )
    kept = pltpu.make_async_copy(gate_ref.at[me], gated_ref.at[me], local_sem.at[0])
    kept.start()

    @pl.when(jnp.logical_not(has_above))
    def _():
        above[...] = jnp.zeros_like(above)
        above_note[...] = jnp.zeros_like(above_note)

    @pl.when(jnp.logical_not(has_below))
    def _():
        below[...] = jnp.zeros_like(below)
        below_note[...] = jnp.zeros_like(below_note)

    pl.when(has_above)(
        lambda: remote(
            above_note, above_note, tell_send.at[0], tell_recv.at[0], me, t - 1
        ).wait_recv()
    )
    pl.when(has_below)(
        lambda: remote(
            below_note, below_note, tell_send.at[1], tell_recv.at[1], me, t + 1
        ).wait_recv()
    )

    def rims(s):
        pl.when(has_above)(
            lambda: remote(
                above.at[s], above.at[s], above_send.at[s], above_recv.at[s], me, t - 1
            ).wait_recv()
        )
        pl.when(has_below)(
            lambda: remote(
                below.at[s], below.at[s], below_send.at[s], below_recv.at[s], me, t + 1
            ).wait_recv()
        )

    def wide(ref, *at):
        return ref[at].astype(jnp.float32)

    def row(s, f):
        value = wide(terms_ref, s, 0, f)
        for note, items in ((above_note, above), (below_note, below)):
            for c in range(CAP):
                place = note[s, c : c + 1, :]
                place = jnp.concatenate([place] * (value.shape[1] // place.shape[1]), axis=1)
                here = jnp.broadcast_to(place, value.shape) == f.astype(jnp.float32)
                value = value + jnp.where(here, wide(items, s, c), 0.0)
        return value

    for k, zs in enumerate(ring):
        for j in range(1, across):
            xs = (x + j) % across
            s = zs * across + xs
            rims(s)

            @pl.loop(0, frames)
            def _(f):
                side_out[j - 1, k, 0, f] = row(s, f).astype(jnp.bfloat16)
                side_out[j - 1, k, 1, f] = terms_ref[s, 1, f]

            launch(
                lambda k=k, j=j, xs=xs: remote(
                    side_out.at[j - 1, k],
                    side_in.at[j - 1, k],
                    side_send.at[j - 1, k],
                    side_recv.at[j - 1, k],
                    z * across + xs,
                    t,
                )
            )

    def mated(k, p):
        part = pl.ds(p * length, length)
        for j in range(1, cores):
            remote(
                mate_in.at[k, j - 1, part], mate_in.at[k, j - 1, part],
                mate_send.at[k, j - 1, p], mate_recv.at[k, j - 1, p],
                me, y * cores + (core + j) % cores,
            ).wait_recv()

    for k, ys in enumerate(bands[:-1]):
        for p in range(pieces):
            mated(k, p)

            @pl.loop(p * length, (p + 1) * length)
            def _(i):
                value = wide(bank_ref, ys * cores + core, i)
                for j in range(1, cores):
                    value = value + wide(mate_in, k, j - 1, i)
                band_out[k, i] = value.astype(jnp.bfloat16)

            launch(
                lambda k=k, p=p, ys=ys: remote(
                    band_out.at[k, pl.ds(p * length, length)],
                    band_in.at[k, pl.ds(p * length, length)],
                    band_send.at[k, p], band_recv.at[k, p],
                    me, ys * cores + core,
                )
            )

    for k, zs in enumerate(ring):
        s = zs * across + x
        rims(s)
        for j in range(1, across):
            remote(
                side_in.at[j - 1, k], side_in.at[j - 1, k],
                side_send.at[j - 1, k], side_recv.at[j - 1, k],
                z * across + (x + j) % across, t,
            ).wait_recv()

        def summed(f):
            first, second = row(s, f), wide(terms_ref, s, 1, f)
            for j in range(1, across):
                first = first + wide(side_in, j - 1, k, 0, f)
                second = second + wide(side_in, j - 1, k, 1, f)
            return first, second

        if k < deep - 1:

            @pl.loop(0, frames)
            def _(f):
                first, second = summed(f)
                far_out[k, 0, f] = first.astype(jnp.bfloat16)
                far_out[k, 1, f] = second.astype(jnp.bfloat16)

            launch(
                lambda k=k, zs=zs: remote(
                    far_out.at[k], far_in.at[k], far_send.at[k], far_recv.at[k],
                    zs * across + x, t,
                )
            )
        else:

            @pl.loop(0, frames)
            def _(f):
                first, second = summed(f)
                total[0, f] = wide(own_ref, 1, f) + first
                total[1, f] = wide(own_ref, 0, f) + second

    for k in range(deep - 1):
        remote(
            far_in.at[k], far_in.at[k], far_send.at[k], far_recv.at[k], ring[k] * across + x, t
        ).wait_recv()

    @pl.loop(0, frames)
    def _(f):
        first, second = total[0, f], total[1, f]
        for k in range(deep - 1):
            first = first + wide(far_in, k, 0, f)
            second = second + wide(far_in, k, 1, f)
        input_ref[f] = first.astype(jnp.bfloat16)
        result_ref[f] = second.astype(jnp.bfloat16)

    for p in range(pieces):
        mated(high - 1, p)
        for k in range(high - 1):
            part = pl.ds(p * length, length)
            remote(
                band_in.at[k, part], band_in.at[k, part], band_send.at[k, p], band_recv.at[k, p],
                me, bands[k] * cores + core,
            ).wait_recv()

        @pl.loop(p * length, (p + 1) * length)
        def _(i):
            value = wide(bank_ref, t, i)
            for j in range(1, cores):
                value = value + wide(mate_in, high - 1, j - 1, i)
            for k in range(high - 1):
                value = value + wide(band_in, k, i)
            grad_ref[i] = value

    for j in range(1, owners):
        s = (me + owners - j) % owners
        remote(
            gate_ref.at[s], gated_ref.at[s], gate_send.at[j - 1], gate_recv.at[j - 1], s, t
        ).wait_recv()
    for cond, make in started:
        if cond is None:
            make().wait_send()
        else:
            pl.when(cond)(lambda make=make: make().wait_send())
    kept.wait()


def collect(terms, edges, notes, gates, bank, own):
    owners, _, frames, columns, channels = terms.shape
    tiles, steps, share, _ = bank.shape
    deep, across = grid_of(owners)
    cores = 1 if tiles % 2 else 2
    high = tiles // cores
    dma = pltpu.SemaphoreType.DMA
    vmem = pl.BlockSpec(memory_space=pltpu.VMEM)
    beside, past, mates, far = (max(v - 1, 1) for v in (across, deep, cores, high))
    block = (2, frames, columns, channels)
    pieces = 4 if steps % 4 == 0 else 1

    def room(*shape):
        return pltpu.VMEM(shape, jnp.bfloat16)

    return pl.pallas_call(
        functools.partial(collect_kernel, deep, across, high, cores),
        out_shape=[
            jax.ShapeDtypeStruct(block[1:], jnp.bfloat16),
            jax.ShapeDtypeStruct(block[1:], jnp.bfloat16),
            jax.ShapeDtypeStruct(gates.shape, gates.dtype),
            jax.ShapeDtypeStruct(bank.shape[1:], jnp.float32),
        ],
        in_specs=[vmem] * 6,
        out_specs=[vmem] * 4,
        scratch_shapes=[
            room(owners, *edges.shape[2:]),
            room(owners, *edges.shape[2:]),
            pltpu.VMEM(notes.shape, jnp.float32),
            pltpu.VMEM(notes.shape, jnp.float32),
            room(beside, deep, *block),
            room(beside, deep, *block),
            room(past, *block),
            room(past, *block),
            pltpu.VMEM(block, jnp.float32),
            room(high, mates, steps, share, channels),
            room(far, steps, share, channels),
            room(far, steps, share, channels),
            dma((1,)),
            dma((owners,)), dma((owners,)), dma((owners,)), dma((owners,)),
            dma((beside, deep)), dma((beside, deep)),
            dma((past,)), dma((past,)),
            dma((high, mates, pieces)), dma((high, mates, pieces)),
            dma((far, pieces)), dma((far, pieces)),
            dma((max(owners - 1, 1),)), dma((max(owners - 1, 1),)),
            dma((2,)), dma((2,)),
        ],
        compiler_params=pltpu.CompilerParams(
            collective_id=1, has_side_effects=True, vmem_limit_bytes=56 * 1024 * 1024
        ),
        name="collect",
    )(terms, edges, notes, gates, bank, own)


def shards(frames, kernels, experts, counts, gate_weights, cotangent):
    owners = lax.axis_size("dp")
    tiles = lax.axis_size("tile")
    local = kernels.shape[0]
    chosen = experts[:, 0]
    frame_count, slots = chosen.shape
    active = jnp.arange(slots)[None, :] < counts[:, 0][:, None]
    owner_of = chosen // local
    hit = (owner_of[:, :, None] == jnp.arange(owners)) & active[:, :, None]
    wanted = jnp.any(hit, axis=1)
    position = jnp.cumsum(wanted.astype(jnp.int32), axis=0) - 1
    slot_map = wanted.T[:, None, :] & (
        position.T[:, None, :] == jnp.arange(CAP)[None, :, None]
    )
    request = jnp.max(jnp.where(hit, (chosen % local)[:, :, None], 0), axis=(0, 1))
    tile_gate = jnp.sum(jnp.where(hit, gate_weights[:, 0][:, :, None], 0.0), axis=1)
    weight = jnp.sum(jnp.where(slot_map, tile_gate.T[:, None, :], 0.0), axis=2)
    place = jnp.sum(
        jnp.where(slot_map, jnp.arange(frame_count)[None, None, :], 0), axis=2
    )
    note = jnp.concatenate(
        [request[:, None].astype(jnp.float32), weight, place.astype(jnp.float32)], axis=1
    )
    note = jnp.pad(note[:, None, :], ((0, 0), (0, 7), (0, 128 - note.shape[1])))
    own = jnp.stack([frames[:, 0], cotangent[:, 0]])
    rows, above, below, noted = spread(own, note, owners, tiles)
    noted = noted[:, 0]
    pick = noted[:, 0].astype(jnp.int32)
    shares = noted[:, 1 : 1 + CAP]
    places = noted[:, 1 + CAP : 1 + 2 * CAP].astype(jnp.int32)
    t = lax.axis_index("tile")
    rim = jnp.stack([t > 0, t < tiles - 1]).astype(jnp.int32)

    spots = jnp.broadcast_to(places.astype(jnp.float32)[:, :, None], (owners, CAP, 128))
    spots = jnp.pad(spots, ((0, 0), (0, 8 - CAP), (0, 0)))
    back, edges, gates, bank_grad = owner(
        pick, shares, places, rim, rows, above, below, kernels, tiles
    )
    result, input_grad, gated, bank_part = collect(back, edges, spots, gates, bank_grad, own)
    kernel_part = jnp.swapaxes(bank_part, 1, 2).reshape(
        kernels.shape[:3] + (bank_part.shape[1],)
    )
    gated = gated[:, :CAP, 0]
    selected = jnp.sum(jnp.where(slot_map, gated[:, :, None], 0.0), axis=1)
    gate_grad = jnp.sum(jnp.where(hit, selected.T[:, None, :], 0.0), axis=2)
    return (result[:, None], input_grad[:, None], gate_grad[:, None, :], kernel_part)


def solution(mesh):
    return jax.shard_map(
        shards,
        mesh=mesh,
        in_specs=(
            P("dp", "tile", None, None),
            P("dp", None, None, None),
            P("dp", "tile", None),
            P("dp", "tile"),
            P("dp", "tile", None),
            P("dp", "tile", None, None),
        ),
        out_specs=(
            P("dp", "tile", None, None),
            P("dp", "tile", None, None),
            P("dp", "tile", None),
            P("dp", None, None, "tile"),
        ),
        check_vma=False,
    )
```

profile of v0, /device:TPU:0, one launch (start us, length us, event | category | flops | bytes accessed | tf_op | source)
XLA Modules:
  0.0 106.7 jit_solution(1535604957784884319)
XLA Ops:
  0.6 0.7 add_select_fusion.1
  1.3 0.7 iota_compare_fusion.2
  2.0 0.1 select_reduce_fusion.2
  2.2 0.8 select_reduce_fusion.1
  3.1 0.1 copy.31
  3.2 1.0 pad_maximum_fusion.own_ref
  4.2 0.0 copy-start
  4.2 31.0 %spread.1 = (bf16[8,2,4,64,256]{4,3,2,1,0:T(8,128)(2,1)S(1)}, bf16[8,4,64,256]{3,2,1,0:T(8,128)(2,1)S(1)}, bf16[8,4,64,256]{3,2,1,0:T(8,128)(2,1)S(1)}, f32[8,8,128]{2,1,0:T(8,128)S(1)}) custom-call(bf16[2,4,64,256]{3,2,1,0:T(8,128)(2,1)S(1)} %pad_maximum_fusion.own_ref, f32[8,8,128]{2,1,0:T(8,128)S(1)} %pad.8.note_ref), custom_call_target="tpu_custom_call" | custom-call | tf_op jit(solution)/shard_map/spread/pallas_call | solution.py:345
  35.2 0.0 copy-start.1
  35.2 1.3 %copy-done.1 = bf16[8,2,4,64,256]{4,3,2,1,0:T(8,128)(2,1)} copy-done((bf16[8,2,4,64,256]{4,3,2,1,0:T(8,128)(2,1)}, bf16[8,2,4,64,256]{4,3,2,1,0:T(8,128)(2,1)S(1)}, u32[]{:S(2)}) %copy-start.1) | copy-done | bytes 2097176
  36.5 0.1 fusion.3
  36.6 0.1 convert_reduce_fusion.pick_ref
  36.7 0.1 add_convert_fusion.rim_ref
  36.8 15.5 %owner.1 = (bf16[8,2,4,64,256]{4,3,2,1,0:T(8,128)(2,1)S(1)}, bf16[8,2,2,64,256]{4,3,2,1,0:T(8,128)(2,1)S(1)}, f32[8,8,128]{2,1,0:T(8,128)S(1)}, bf16[4,36,64,256]{3,2,1,0:T(8,128)(2,1)}) custom-call(s32[8]{0:T(128)S(1)} %convert_reduce_fusion.pick_ref, f32[8,2]{1,0:T(8,128)S(1)} %get-tuple-element.46.weight_ref, s32[8,2]{1,0:T(8,128)S(1)} %get-tuple-element.45.place_ref, ...), custom_call_target="tpu_custom_call" | custom-call | tf_op jit(solution)/shard_map/owner/pallas_call | solution.py:146
  52.3 0.0 copy-done
  52.3 0.0 copy-start.2
  52.3 1.3 %copy-done.2 = bf16[8,2,4,64,256]{4,3,2,1,0:T(8,128)(2,1)} copy-done((bf16[8,2,4,64,256]{4,3,2,1,0:T(8,128)(2,1)}, bf16[8,2,4,64,256]{4,3,2,1,0:T(8,128)(2,1)S(1)}, u32[]{:S(2)}) %copy-start.2) | copy-done | bytes 2097176
  53.7 0.0 copy-start.3
  53.7 1.0 copy-done.3
  54.6 0.0 copy-start.4
  54.6 0.6 copy-done.4
  55.2 0.1 broadcast_in_dim.112
  55.3 0.6 pad.9.note_ref
  55.9 42.7 %collect.1 = (bf16[4,64,256]{2,1,0:T(8,128)(2,1)}, bf16[4,64,256]{2,1,0:T(8,128)(2,1)}, f32[8,8,128]{2,1,0:T(8,128)}, f32[36,64,256]{2,1,0:T(8,128)}) custom-call(bf16[8,2,4,64,256]{4,3,2,1,0:T(8,128)(2,1)} %copy-done.2, bf16[8,2,2,64,256]{4,3,2,1,0:T(8,128)(2,1)} %copy-done.3, f32[8,8,128]{2,1,0:T(8,128)} %pad.9.note_ref, f32[8,8,128]{2,1,0:T(8,128)} %copy-done.4, ...), custom_call_target="tpu_custom_call" | custom-call | tf_op jit(solution)/shard_map/collect/pallas_call | solution.py:649
  98.7 0.8 slice.19
  99.4 0.1 copy.33
  99.5 0.7 select_reduce_fusion
  100.2 1.6 %copy.42 = bf16[4,1,64,256]{3,2,1,0:T(8,128)(2,1)} copy(bf16[4,1,64,256]{3,2,1,0:T(8,128)(2,1)} %bitcast.33) | data formatting | bytes 262144
  101.8 1.6 %copy.43 = bf16[4,1,64,256]{3,2,1,0:T(8,128)(2,1)} copy(bf16[4,1,64,256]{3,2,1,0:T(8,128)(2,1)} %bitcast.32) | data formatting | bytes 262144
  103.3 3.3 %copy.44 = f32[4,9,256,64]{2,3,1,0:T(8,128)} copy(f32[4,9,256,64]{2,3,1,0:T(8,128)} %bitcast.31) | data formatting | bytes 4718592
  (13 shorter events, 0.2 us)
Async XLA Ops:
  4.2 48.2 %copy-start = (bf16[2,4,64,256]{3,2,1,0:T(8,128)(2,1)}, bf16[2,4,64,256]{3,2,1,0:T(8,128)(2,1)S(1)}, u32[]{:S(2)}) copy-start(bf16[2,4,64,256]{3,2,1,0:T(8,128)(2,1)S(1)} %pad_maximum_fusion.own_ref) | copy-start | bytes 786436
  35.2 1.3 %copy-start.1 = (bf16[8,2,4,64,256]{4,3,2,1,0:T(8,128)(2,1)}, bf16[8,2,4,64,256]{4,3,2,1,0:T(8,128)(2,1)S(1)}, u32[]{:S(2)}) copy-start(bf16[8,2,4,64,256]{4,3,2,1,0:T(8,128)(2,1)S(1)} %get-tuple-element.17.rows_ref) | copy-start | bytes 6291460
  52.3 1.3 %copy-start.2 = (bf16[8,2,4,64,256]{4,3,2,1,0:T(8,128)(2,1)}, bf16[8,2,4,64,256]{4,3,2,1,0:T(8,128)(2,1)S(1)}, u32[]{:S(2)}) copy-start(bf16[8,2,4,64,256]{4,3,2,1,0:T(8,128)(2,1)S(1)} %get-tuple-element.20.terms_ref) | copy-start | bytes 6291460
  53.7 1.0 copy-start.3
  54.6 0.6 copy-start.4
where the time goes:
time: 107 us
  Pallas kernels  89.3 us (83%)
  local copies, waits for them, and re-layouts  12.3 us (11%)
  other arithmetic  4.36 us (4%)
    pallas_call x1, Pallas kernels, collect(): pl.pallas_call(functools.partial(collect_kernel, deep, across, high, core...  42.7 us
    pallas_call x1, Pallas kernels, spread(): pl.pallas_call(functools.partial(spread_kernel, deep, across, tiles), out...  31 us
    pallas_call x1, Pallas kernels, owner(): pl.pallas_call(owner_kernel, grid_spec=spec, out_shape=[jax.ShapeDtypeStr...  15.5 us
    unnamed x13, local copies, waits for them, and re-layouts  10.7 us

commit v1 on v0

v1 whole, which is shorter than its diff:
```python
import functools
from types import SimpleNamespace

import jax
import jax.numpy as jnp
from jax import lax
from jax.experimental import pallas as pl
from jax.experimental.pallas import tpu as pltpu
from jax.sharding import PartitionSpec as P

CAP = 2


def grid_of(owners):
    across = 1
    while across * across * 4 <= owners:
        across *= 2
    while owners % across:
        across -= 1
    return owners // across, across


def remote(src, dst, send, recv, dp, tile):
    return pltpu.make_async_remote_copy(
        src_ref=src,
        dst_ref=dst,
        send_sem=send,
        recv_sem=recv,
        device_id=(dp, tile),
        device_id_type=pl.DeviceIdType.MESH,
    )


def go(copy):
    copy.start()


def drain(copy):
    copy.wait_send()


def layer_kernel(
    deep, across, high, cores, names,
    frames_ref, cot_ref, note_ref, weight_ref, bank_hbm,
    result_ref, input_ref, gated_ref, grad_ref, *rest,
):
    v = SimpleNamespace(**dict(zip(names, rest)))
    me, t = lax.axis_index("dp"), lax.axis_index("tile")
    z, x = me // across, me % across
    y, core = t // cores, t % cores
    owners, tiles = deep * across, high * cores
    frames, columns, channels = frames_ref.shape
    experts, taps, share, _ = grad_ref.shape
    cap = CAP
    rows = cap * columns
    has_above, has_below = t > 0, t < tiles - 1
    t_above, t_below = (t + tiles - 1) % tiles, (t + 1) % tiles
    bf16, f32 = jnp.bfloat16, jnp.float32

    load_bank = pltpu.make_async_copy(bank_hbm, v.bank, v.local_sem.at[0])
    load_bank.start()

    barrier = pltpu.get_barrier_semaphore()
    for j in range(1, owners):
        pl.semaphore_signal(
            barrier, device_id=((me + j) % owners, t), device_id_type=pl.DeviceIdType.MESH
        )
    for j in range(1, tiles):
        pl.semaphore_signal(
            barrier, device_id=(me, (t + j) % tiles), device_id_type=pl.DeviceIdType.MESH
        )
    pl.semaphore_wait(barrier, owners - 1 + tiles - 1)

    def lift(act, s, fr, co):
        act(remote(fr, v.f.at[s, t], v.f_up.at[s], v.f_recv.at[s], me + across, t))
        act(remote(co, v.c.at[s], v.c_up.at[s], v.c_recv.at[s], me + across, t))

    def sink(act, s, fr, co):
        act(remote(fr, v.f.at[s, t], v.f_down.at[s], v.f_recv.at[s], me - across, t))
        act(remote(co, v.c.at[s], v.c_down.at[s], v.c_recv.at[s], me - across, t))

    def side_frames(act, s, fr):
        for j in range(1, across):
            act(
                remote(
                    fr, v.f.at[s, t], v.f_side.at[j - 1, s], v.f_recv.at[s],
                    z * across + (x + j) % across, t,
                )
            )

    def side_packed(act, s, zs):
        for j in range(1, across):
            act(
                remote(
                    v.cpo.at[j - 1, zs], v.cp.at[s], v.cp_send.at[j - 1, zs], v.cp_recv.at[s],
                    z * across + (x + j) % across, t,
                )
            )

    def tile_frames(act, s, fr):
        for j in range(1, cores):
            act(
                remote(
                    fr, v.f.at[s, t], v.mate_send.at[j - 1, s], v.ft_recv.at[s, t],
                    me, y * cores + (core + j) % cores,
                )
            )
        for j in range(1, high):
            act(
                remote(
                    fr, v.f.at[s, t], v.far_tile.at[j - 1, s], v.ft_recv.at[s, t],
                    me, (y + j) % high * cores + core,
                )
            )

    def pass_on(act, s, j):
        tt = (y + j) % high * cores + core
        for i in range(1, cores):
            act(
                remote(
                    v.f.at[s, tt], v.f.at[s, tt], v.pass_send.at[j - 1, i - 1, s],
                    v.ft_recv.at[s, tt], me, y * cores + (core + i) % cores,
                )
            )

    def edge_down(act, s):
        act(
            remote(
                v.eo.at[s, 1], v.above.at[s], v.above_send.at[s], v.above_recv.at[s], me, t + 1
            )
        )

    def edge_up(act, s):
        act(
            remote(
                v.eo.at[s, 0], v.below.at[s], v.below_send.at[s], v.below_recv.at[s], me, t - 1
            )
        )

    def slices(act, s):
        for j in range(1, tiles):
            tt = (t + j) % tiles
            act(
                remote(
                    v.go.at[s, tt], v.gi.at[s, t], v.g_send.at[j - 1, s], v.g_recv.at[s, t], me, tt
                )
            )

    def gates(act, s):
        act(
            remote(
                v.gate.at[s], gated_ref.at[me], v.gate_send.at[s], v.gate_recv.at[me], s, t
            )
        )

    def side_terms(act, s, zs, xj):
        act(
            remote(
                v.sbo.at[xj - 1, zs], v.sbi.at[xj - 1, zs],
                v.sb_send.at[xj - 1, zs], v.sb_recv.at[xj - 1, zs], z * across + s % across, t,
            )
        )
        act(
            remote(
                v.act.at[s], v.sai.at[xj - 1, zs],
                v.sa_send.at[xj - 1, zs], v.sa_recv.at[xj - 1, zs], z * across + s % across, t,
            )
        )

    def far_terms(act, zs):
        act(
            remote(
                v.fo.at[zs], v.fi.at[z], v.fo_send.at[zs], v.fi_recv.at[z], zs * across + x, t
            )
        )

    def received(ref, sem):
        remote(ref, ref, v.spare_sem.at[0], sem, me, t).wait_recv()

    def send_notes(act):
        for j in range(1, owners):
            peer = (me + j) % owners
            act(
                remote(
                    note_ref.at[pl.ds(peer // across * across, across)], v.n.at[me],
                    v.note_send.at[0, j - 1], v.note_recv.at[0, me], peer, t,
                )
            )
            act(
                remote(
                    weight_ref.at[peer], v.w.at[me],
                    v.note_send.at[1, j - 1], v.note_recv.at[1, me], peer, t,
                )
            )

    send_notes(go)
    own_notes = pltpu.make_async_copy(
        note_ref.at[pl.ds(z * across, across)], v.n.at[me], v.local_sem.at[1]
    )
    own_notes.start()
    own_weights = pltpu.make_async_copy(weight_ref.at[me], v.w.at[me], v.local_sem.at[2])
    own_weights.start()
    own_rows = pltpu.make_async_copy(frames_ref, v.f.at[me, t], v.local_sem.at[3])
    own_rows.start()
    pl.when(z < deep - 1)(lambda: lift(go, me, frames_ref, cot_ref))
    pl.when(z > 0)(lambda: sink(go, me, frames_ref, cot_ref))
    side_frames(go, me, frames_ref)
    tile_frames(go, me, frames_ref)

    @pl.when(jnp.logical_not(has_above))
    def _():
        v.above[...] = jnp.zeros_like(v.above)

    @pl.when(jnp.logical_not(has_below))
    def _():
        v.below[...] = jnp.zeros_like(v.below)

    own_notes.wait()
    own_weights.wait()
    for j in range(1, owners):
        s = (me + j) % owners
        received(v.n.at[s], v.note_recv.at[0, s])
        received(v.w.at[s], v.note_recv.at[1, s])

    def tile_notes(act):
        for j in range(1, tiles):
            act(
                remote(
                    v.n, v.tn.at[t], v.tn_send.at[j - 1], v.tn_recv.at[t], me, (t + j) % tiles
                )
            )

    tile_notes(go)
    copies = [
        pltpu.make_async_copy(v.n, v.tn.at[t], v.local_sem.at[1]),
        pltpu.make_async_copy(v.n, v.ns, v.local_sem.at[2]),
        pltpu.make_async_copy(v.w, v.ws, v.local_sem.at[4]),
    ]
    for copy in copies:
        copy.start()
    for copy in copies:
        copy.wait()

    def places(s, xo):
        return [v.ns[s, xo, 0, 1 + c] for c in range(cap)]

    def tile_places(tt, s):
        return [v.ts[tt, s, x, 0, 1 + c] for c in range(cap)]

    def picked(spots, load):
        parts = []
        for c in range(cap):
            value = jnp.zeros((columns, channels), bf16)
            for f in range(frames):
                value = jnp.where(spots[c] == f, load(f), value)
            parts.append(value)
        return parts

    def pack(s, zs, load):
        for j in range(1, across):
            parts = picked(places(s, (x + j) % across), load)
            for c in range(cap):
                v.cpo[j - 1, zs, c] = parts[c]
        parts = picked(places(s, x), load)
        for c in range(cap):
            v.cp[s, c] = parts[c]
        side_packed(go, s, zs)

    pack(me, z, lambda f: cot_ref[f])

    for j in range(1, tiles):
        tt = (t + j) % tiles
        received(v.tn.at[tt], v.tn_recv.at[tt])
    tile_scalars = pltpu.make_async_copy(v.tn, v.ts, v.local_sem.at[1])
    tile_scalars.start()
    tile_scalars.wait()
    own_rows.wait()
    load_bank.wait()

    count = (2 * deep - 1) * across

    def stage(n, body, lead=None):
        j, xj = n // across, n % across
        zs = z + (j + 1) // 2 * (1 - 2 * (j % 2))
        s = zs * across + (x + xj) % across
        cond = jnp.logical_and(
            jnp.logical_and(n >= 0, n < count), jnp.logical_and(zs >= 0, zs < deep)
        )
        if lead is True:
            cond = jnp.logical_and(cond, xj == 0)
        elif lead is False:
            cond = jnp.logical_and(cond, xj > 0)
        pl.when(cond)(lambda: body(s, zs, xj))

    def arrive(s, zs, xj):
        received(v.f.at[s, t], v.f_recv.at[s])

        @pl.when(xj == 0)
        def _():
            received(v.c.at[s], v.c_recv.at[s])
            pl.when(jnp.logical_and(zs < z, z < deep - 1))(
                lambda: lift(go, s, v.f.at[s, t], v.c.at[s])
            )
            pl.when(jnp.logical_and(zs > z, z > 0))(
                lambda: sink(go, s, v.f.at[s, t], v.c.at[s])
            )
            side_frames(go, s, v.f.at[s, t])
            pack(s, zs, lambda f: v.c[s, f])

        @pl.when(xj > 0)
        def _():
            received(v.cp.at[s], v.cp_recv.at[s])

        tile_frames(go, s, v.f.at[s, t])

    def across_tiles(s, zs, xj):
        for j in range(1, high):
            tt = (y + j) % high * cores + core
            received(v.f.at[s, tt], v.ft_recv.at[s, tt])
            pass_on(go, s, j)

    place = lax.broadcasted_iota(jnp.int32, (rows, 1), 0)
    item = place // columns
    column = place % columns

    def later(value):
        return jnp.where(column == 0, 0.0, pltpu.roll(value, 1, 0))

    def sooner(value):
        return jnp.where(column == columns - 1, 0.0, pltpu.roll(value, rows - 1, 0))

    def compute(s, zs, xj):
        for j in range(high):
            for i in range(1, cores):
                tt = (y + j) % high * cores + (core + i) % cores
                received(v.f.at[s, tt], v.ft_recv.at[s, tt])
        e = v.ns[s, x, 0, 0]
        spots = places(s, x)
        blank = jnp.zeros((rows, channels), bf16)

        def gather(tt):
            return jnp.concatenate(picked(spots, lambda f: v.f[s, tt, f]), axis=0)

        window = [
            jnp.where(has_above, gather(t_above), blank),
            gather(t),
            jnp.where(has_below, gather(t_below), blank),
        ]
        upstream = v.cp[s].reshape(rows, channels).astype(f32)
        weight = jnp.zeros((rows, 1), f32)
        for c in range(cap):
            weight = jnp.where(item == c, v.ws[s, 0, c], weight)

        def column_term(db):
            total = jnp.dot(window[0], v.bank[e, db], preferred_element_type=f32)
            for da in (1, 2):
                total = total + jnp.dot(
                    window[da], v.bank[e, 3 * da + db], preferred_element_type=f32
                )
            return total

        pre = column_term(1) + later(column_term(0)) + sooner(column_term(2))
        pre = pre.astype(bf16).astype(f32)
        squash = jax.nn.sigmoid(pre)
        activated = pre * squash
        slope = squash * (1.0 + pre * (1.0 - squash))
        v.act[s] = (weight * activated).astype(bf16).reshape(cap, columns, channels)
        sums = jnp.sum((upstream * activated).reshape(cap, columns, channels), axis=1)
        sums = jnp.broadcast_to(jnp.sum(sums, axis=1, keepdims=True), (cap, 128))
        sums = jnp.concatenate([sums, jnp.zeros((8 - cap, 128), f32)], axis=0)
        v.gate[s] = sums

        @pl.when(s != me)
        def _():
            gates(go, s)

        @pl.when(s == me)
        def _():
            gated_ref[me] = sums

        grad = (upstream * weight * slope).astype(bf16)
        turned = jnp.transpose(grad.astype(f32)).astype(bf16)
        for k in range(tiles):
            v.go[s, k] = turned[k * share : (k + 1) * share]
        v.gi[s, t] = v.go[s, t]
        slices(go, s)
        for da in (0, 2, 1):
            parts = [
                lax.dot_general(
                    grad,
                    v.bank[e, 3 * da + db],
                    (((1,), (1,)), ((), ())),
                    preferred_element_type=f32,
                )
                for db in range(3)
            ]
            total = parts[1] + sooner(parts[0]) + later(parts[2])
            total = total.astype(bf16).reshape(cap, columns, channels)
            if da == 1:
                v.bk[s] = total
            else:
                v.eo[s, da // 2] = total
        pl.when(has_above)(lambda: edge_up(go, s))
        pl.when(has_below)(lambda: edge_down(go, s))

    def rims(s):
        pl.when(has_above)(lambda: received(v.above.at[s], v.above_recv.at[s]))
        pl.when(has_below)(lambda: received(v.below.at[s], v.below_recv.at[s]))

    def spread_out(value, spots, load, f):
        for c in range(cap):
            value = value + jnp.where(spots[c] == f, load(c).astype(f32), 0.0)
        return value

    def back_rows(s):
        mine = places(s, x)
        upper = [jnp.where(has_above, p, -1) for p in tile_places(t_above, s)]
        lower = [jnp.where(has_below, p, -1) for p in tile_places(t_below, s)]

        def row(f):
            value = jnp.zeros((columns, channels), f32)
            value = spread_out(value, mine, lambda c: v.bk[s, c], f)
            value = spread_out(value, upper, lambda c: v.above[s, c], f)
            return spread_out(value, lower, lambda c: v.below[s, c], f)

        return row

    def to_side(s, zs, xj):
        rims(s)
        row = back_rows(s)
        for f in range(frames):
            v.sbo[xj - 1, zs, f] = row(f).astype(bf16)
        side_terms(go, s, zs, xj)

    def to_far(s, zs, xj):
        rims(s)
        for j in range(1, across):
            received(v.sbi.at[j - 1, zs], v.sb_recv.at[j - 1, zs])
            received(v.sai.at[j - 1, zs], v.sa_recv.at[j - 1, zs])
        row = back_rows(s)
        spots = [places(s, x)] + [places(s, (x + across - j) % across) for j in range(1, across)]
        for f in range(frames):
            first = row(f)
            second = spread_out(
                jnp.zeros((columns, channels), f32), spots[0], lambda c: v.act[s, c], f
            )
            for j in range(1, across):
                first = first + v.sbi[j - 1, zs, f].astype(f32)
                second = spread_out(second, spots[j], lambda c: v.sai[j - 1, zs, c], f)
            v.total[0, f] = first
            v.total[1, f] = second

        @pl.when(zs == z)
        def _():
            for f in range(frames):
                v.base[0, f] = v.total[0, f] + cot_ref[f].astype(f32)
                v.base[1, f] = v.total[1, f] + frames_ref[f].astype(f32)

        @pl.when(zs != z)
        def _():
            v.fo[zs] = v.total[...].astype(bf16)
            far_terms(go, zs)

    @pl.loop(0, count + across + 3)
    def _(n):
        stage(n - 2, compute)
        stage(n - 3, to_side, lead=False)
        stage(n - across - 3, to_far, lead=True)
        stage(n - 1, across_tiles)
        pl.when(n > 0)(lambda: stage(n, arrive))

    @pl.loop(0, experts)
    def _(k):
        grad_ref[k] = jnp.zeros_like(grad_ref[k])

    lane = lax.broadcasted_iota(jnp.int32, (1, rows), 1) % columns

    @pl.loop(0, owners)
    def _(i):
        s = (me + i) % owners
        for j in range(1, tiles):
            tt = (t + j) % tiles
            received(v.gi.at[s, tt], v.g_recv.at[s, tt])
        for tt in range(tiles):
            e = v.ts[tt, s, x, 0, 0]
            spots = tile_places(tt, s)
            span = slice(tt * rows, (tt + 1) * rows)
            for da in range(3):
                source = tt + da - 1
                if 0 <= source < tiles:
                    parts = picked(spots, lambda f: v.f[s, source, f])
                    v.xw[da, span] = jnp.concatenate(parts, axis=0)
                else:
                    v.xw[da, span] = jnp.zeros((rows, channels), bf16)
            g = v.gi[s, tt].astype(f32)
            moved = [
                jnp.where(lane == columns - 1, 0.0, pltpu.roll(g, rows - 1, 1)).astype(bf16),
                v.gi[s, tt],
                jnp.where(lane == 0, 0.0, pltpu.roll(g, 1, 1)).astype(bf16),
            ]
            for db in range(3):
                for k in range(experts):
                    v.gt[db, k * share : (k + 1) * share, span] = jnp.where(
                        e == k, moved[db], jnp.zeros_like(moved[db])
                    )
        for da in range(3):
            for db in range(3):
                term = jnp.dot(v.gt[db], v.xw[da], preferred_element_type=f32)
                grad_ref[:, 3 * da + db] += term.reshape(experts, share, channels)

    for k in range(1, deep):
        zs = (z + k) % deep
        received(v.fi.at[zs], v.fi_recv.at[zs])
    for f in range(frames):
        first, second = v.base[0, f], v.base[1, f]
        for k in range(1, deep):
            zs = (z + k) % deep
            first = first + v.fi[zs, 0, f].astype(f32)
            second = second + v.fi[zs, 1, f].astype(f32)
        input_ref[f] = first.astype(bf16)
        result_ref[f] = second.astype(bf16)

    for j in range(1, owners):
        s = (me + j) % owners
        received(gated_ref.at[s], v.gate_recv.at[s])
        gates(drain, s)
    send_notes(drain)
    tile_notes(drain)
    pl.when(z < deep - 1)(lambda: lift(drain, me, frames_ref, cot_ref))
    pl.when(z > 0)(lambda: sink(drain, me, frames_ref, cot_ref))

    def finish(s, zs, xj):
        @pl.when(xj == 0)
        def _():
            pl.when(jnp.logical_and(zs < z, z < deep - 1))(
                lambda: lift(drain, s, v.f.at[s, t], v.c.at[s])
            )
            pl.when(jnp.logical_and(zs > z, z > 0))(
                lambda: sink(drain, s, v.f.at[s, t], v.c.at[s])
            )
            side_frames(drain, s, v.f.at[s, t])
            side_packed(drain, s, zs)
            pl.when(zs != z)(lambda: far_terms(drain, zs))

        pl.when(xj > 0)(lambda: side_terms(drain, s, zs, xj))
        tile_frames(drain, s, v.f.at[s, t])
        for j in range(1, high):
            pass_on(drain, s, j)
        slices(drain, s)
        pl.when(has_above)(lambda: edge_up(drain, s))
        pl.when(has_below)(lambda: edge_down(drain, s))

    @pl.loop(0, count)
    def _(n):
        stage(n, finish)


def layer(frames, cot, note, weight, kernels, owners, tiles):
    deep, across = grid_of(owners)
    cores = 1 if tiles % 2 else 2
    high = tiles // cores
    count, columns, channels = frames.shape
    experts, taps, _, outputs = kernels.shape
    share = outputs // tiles
    cap = CAP
    rows = cap * columns
    dma = pltpu.SemaphoreType.DMA
    vmem = pl.BlockSpec(memory_space=pltpu.VMEM)
    bf16, f32, i32 = jnp.bfloat16, jnp.float32, jnp.int32
    beside, mates, far = (max(value - 1, 1) for value in (across, cores, high))
    others, peers = max(owners - 1, 1), max(tiles - 1, 1)
    scratch = dict(
        f=pltpu.VMEM((owners, tiles, count, columns, channels), bf16),
        c=pltpu.VMEM((owners, count, columns, channels), bf16),
        cp=pltpu.VMEM((owners, cap, columns, channels), bf16),
        cpo=pltpu.VMEM((beside, deep, cap, columns, channels), bf16),
        n=pltpu.VMEM((owners, across, 1, 128), i32),
        w=pltpu.VMEM((owners, 1, 128), f32),
        tn=pltpu.VMEM((tiles, owners, across, 1, 128), i32),
        ns=pltpu.SMEM((owners, across, 1, 128), i32),
        ws=pltpu.SMEM((owners, 1, 128), f32),
        ts=pltpu.SMEM((tiles, owners, across, 1, 128), i32),
        bank=pltpu.VMEM(kernels.shape, bf16),
        act=pltpu.VMEM((owners, cap, columns, channels), bf16),
        bk=pltpu.VMEM((owners, cap, columns, channels), bf16),
        eo=pltpu.VMEM((owners, 2, cap, columns, channels), bf16),
        above=pltpu.VMEM((owners, cap, columns, channels), bf16),
        below=pltpu.VMEM((owners, cap, columns, channels), bf16),
        go=pltpu.VMEM((owners, tiles, share, rows), bf16),
        gi=pltpu.VMEM((owners, tiles, share, rows), bf16),
        gate=pltpu.VMEM((owners, 8, 128), f32),
        sbo=pltpu.VMEM((beside, deep, count, columns, channels), bf16),
        sbi=pltpu.VMEM((beside, deep, count, columns, channels), bf16),
        sai=pltpu.VMEM((beside, deep, cap, columns, channels), bf16),
        fo=pltpu.VMEM((deep, 2, count, columns, channels), bf16),
        fi=pltpu.VMEM((deep, 2, count, columns, channels), bf16),
        total=pltpu.VMEM((2, count, columns, channels), f32),
        base=pltpu.VMEM((2, count, columns, channels), f32),
        xw=pltpu.VMEM((3, tiles * rows, channels), bf16),
        gt=pltpu.VMEM((3, experts * share, tiles * rows), bf16),
        local_sem=dma((5,)),
        spare_sem=dma((1,)),
        note_send=dma((2, others)), note_recv=dma((2, owners)),
        tn_send=dma((peers,)), tn_recv=dma((tiles,)),
        f_up=dma((owners,)), f_down=dma((owners,)), f_side=dma((beside, owners)), f_recv=dma((owners,)),
        c_up=dma((owners,)), c_down=dma((owners,)), c_recv=dma((owners,)),
        cp_send=dma((beside, deep)), cp_recv=dma((owners,)),
        mate_send=dma((mates, owners)), far_tile=dma((far, owners)),
        pass_send=dma((far, mates, owners)), ft_recv=dma((owners, tiles)),
        above_send=dma((owners,)), above_recv=dma((owners,)),
        below_send=dma((owners,)), below_recv=dma((owners,)),
        g_send=dma((peers, owners)), g_recv=dma((owners, tiles)),
        gate_send=dma((owners,)), gate_recv=dma((owners,)),
        sb_send=dma((beside, deep)), sb_recv=dma((beside, deep)),
        sa_send=dma((beside, deep)), sa_recv=dma((beside, deep)),
        fo_send=dma((deep,)), fi_recv=dma((deep,)),
    )
    return pl.pallas_call(
        functools.partial(layer_kernel, deep, across, high, cores, tuple(scratch)),
        out_shape=[
            jax.ShapeDtypeStruct(frames.shape, bf16),
            jax.ShapeDtypeStruct(frames.shape, bf16),
            jax.ShapeDtypeStruct((owners, 8, 128), f32),
            jax.ShapeDtypeStruct((experts, taps, share, channels), f32),
        ],
        in_specs=[vmem] * 4 + [pl.BlockSpec(memory_space=pl.ANY)],
        out_specs=[vmem] * 4,
        scratch_shapes=list(scratch.values()),
        compiler_params=pltpu.CompilerParams(
            collective_id=0, has_side_effects=True, vmem_limit_bytes=58 * 1024 * 1024
        ),
        name="layer",
    )(frames, cot, note, weight, kernels)


def shards(frames, kernels, experts, counts, gate_weights, cotangent):
    owners = lax.axis_size("dp")
    tiles = lax.axis_size("tile")
    local = kernels.shape[0]
    chosen = experts[:, 0]
    frame_count, slots = chosen.shape
    active = jnp.arange(slots)[None, :] < counts[:, 0][:, None]
    owner_of = chosen // local
    hit = (owner_of[:, :, None] == jnp.arange(owners)) & active[:, :, None]
    wanted = jnp.any(hit, axis=1)
    position = jnp.cumsum(wanted.astype(jnp.int32), axis=0) - 1
    slot_map = wanted.T[:, None, :] & (
        position.T[:, None, :] == jnp.arange(CAP)[None, :, None]
    )
    request = jnp.max(jnp.where(hit, (chosen % local)[:, :, None], 0), axis=(0, 1))
    tile_gate = jnp.sum(jnp.where(hit, gate_weights[:, 0][:, :, None], 0.0), axis=1)
    weight = jnp.sum(jnp.where(slot_map, tile_gate.T[:, None, :], 0.0), axis=2)
    place = jnp.sum(
        jnp.where(slot_map, jnp.arange(1, frame_count + 1)[None, None, :], 0), axis=2
    ) - 1
    note = jnp.concatenate([request[:, None], place], axis=1).astype(jnp.int32)
    note = jnp.pad(note[:, None, :], ((0, 0), (0, 0), (0, 128 - note.shape[1])))
    weight = jnp.pad(weight[:, None, :], ((0, 0), (0, 0), (0, 128 - CAP)))
    result, input_grad, gated, kernel_part = layer(
        frames[:, 0], cotangent[:, 0], note, weight, kernels, owners, tiles
    )
    kernel_part = jnp.swapaxes(kernel_part, 2, 3)
    gated = gated[:, :CAP, 0]
    selected = jnp.sum(jnp.where(slot_map, gated[:, :, None], 0.0), axis=1)
    gate_grad = jnp.sum(jnp.where(hit, selected.T[:, None, :], 0.0), axis=2)
    return (result[:, None], input_grad[:, None], gate_grad[:, None, :], kernel_part)


def solution(mesh):
    return jax.shard_map(
        shards,
        mesh=mesh,
        in_specs=(
            P("dp", "tile", None, None),
            P("dp", None, None, None),
            P("dp", "tile", None),
            P("dp", "tile"),
            P("dp", "tile", None),
            P("dp", "tile", None, None),
        ),
        out_specs=(
            P("dp", "tile", None, None),
            P("dp", "tile", None, None),
            P("dp", "tile", None),
            P("dp", None, None, "tile"),
        ),
        check_vma=False,
    )
```

time: 107 us -> 110 us (1.028)
  the two profiles are of different devices: /device:TPU:0 before, /device:TPU:1 now
where the time goes in v1:
time: 110 us; the launch traced here: 109 us
  Pallas kernels  96.8 us (88%)
  local copies, waits for them, and re-layouts  8.68 us (8%)
  other arithmetic  3.16 us (3%)
    pallas_call x1, Pallas kernels, layer(): pl.pallas_call(functools.partial(layer_kernel, deep, across, high, cores,...  96.8 us
    unnamed x3, local copies, waits for them, and re-layouts  6.46 us

profile of v1, /device:TPU:1, one launch (start us, length us, event | category | flops | bytes accessed | tf_op | source)
XLA Modules:
  0.0 109.3 jit_solution(8654135076036357271)
XLA Ops:
  0.6 0.7 iota_compare_fusion.2
  1.4 0.7 add_select_fusion
  2.1 0.8 select_reduce_fusion.1
  2.8 0.1 select_reduce_fusion.2
  3.0 0.1 select_reduce_fusion.5
  3.1 0.1 copy.19
  3.2 0.6 pad.8.note_ref
  3.8 0.1 copy.20
  3.9 0.6 pad.9.weight_ref
  4.5 96.8 %layer.1 = (bf16[4,64,256]{2,1,0:T(8,128)(2,1)}, bf16[4,64,256]{2,1,0:T(8,128)(2,1)}, f32[8,8,128]{2,1,0:T(8,128)}, f32[4,9,64,256]{3,2,1,0:T(8,128)}) custom-call(bf16[4,64,256]{2,1,0:T(8,128)(2,1)} %bitcast.26, bf16[4,64,256]{2,1,0:T(8,128)(2,1)} %bitcast.27, s32[8,1,128]{2,1,0:T(1,128)} %pad.8.note_ref, f32[8,1,128]{2,1,0:T(1,128)} %pad.9.weight_ref, ...), custom_call_target="tpu_custom_call" | custom-call | tf_op jit(solution)/shard_map/layer/pallas_call | solution.py:618
  101.3 0.8 slice.3
  102.1 0.1 copy.21
  102.2 0.7 select_reduce_fusion
  102.9 1.6 %copy.28 = bf16[4,1,64,256]{3,2,1,0:T(8,128)(2,1)} copy(bf16[4,1,64,256]{3,2,1,0:T(8,128)(2,1)} %bitcast.29) | data formatting | bytes 262144
  104.4 1.6 %copy.29 = bf16[4,1,64,256]{3,2,1,0:T(8,128)(2,1)} copy(bf16[4,1,64,256]{3,2,1,0:T(8,128)(2,1)} %bitcast.28) | data formatting | bytes 262144
  106.0 3.3 %copy.30 = f32[4,9,256,64]{2,3,1,0:T(8,128)} copy(f32[4,9,256,64]{2,3,1,0:T(8,128)} %bitcast.25) | data formatting | bytes 4718592
  (9 shorter events, 0.1 us)

commit v2 on v1

--- a/solution.py
+++ b/solution.py
@@ -1,4 +1,5 @@
 import functools
+import math
 from types import SimpleNamespace
 
 import jax
@@ -41,7 +42,7 @@
 
 def layer_kernel(
     deep, across, high, cores, names,
-    frames_ref, cot_ref, note_ref, weight_ref, bank_hbm,
+    frames_hbm, cot_hbm, note_ref, weight_ref, bank_hbm,
     result_ref, input_ref, gated_ref, grad_ref, *rest,
 ):
     v = SimpleNamespace(**dict(zip(names, rest)))
@@ -49,7 +50,7 @@
     z, x = me // across, me % across
     y, core = t // cores, t % cores
     owners, tiles = deep * across, high * cores
-    frames, columns, channels = frames_ref.shape
+    _, _, frames, columns, channels = v.f.shape
     experts, taps, share, _ = grad_ref.shape
     cap = CAP
     rows = cap * columns
@@ -58,7 +59,13 @@
     bf16, f32 = jnp.bfloat16, jnp.float32
 
     load_bank = pltpu.make_async_copy(bank_hbm, v.bank, v.local_sem.at[0])
+    own_rows = pltpu.make_async_copy(frames_hbm, v.f.at[me, t], v.local_sem.at[3])
+    own_rows.start()
+    own_cot = pltpu.make_async_copy(cot_hbm, v.c.at[me], v.local_sem.at[5])
+    own_cot.start()
     load_bank.start()
+    own_scalars = pltpu.make_async_copy(note_ref, v.os, v.local_sem.at[4])
+    own_scalars.start()
 
     barrier = pltpu.get_barrier_semaphore()
     for j in range(1, owners):
@@ -71,13 +78,27 @@
         )
     pl.semaphore_wait(barrier, owners - 1 + tiles - 1)
 
-    def lift(act, s, fr, co):
-        act(remote(fr, v.f.at[s, t], v.f_up.at[s], v.f_recv.at[s], me + across, t))
-        act(remote(co, v.c.at[s], v.c_up.at[s], v.c_recv.at[s], me + across, t))
-
-    def sink(act, s, fr, co):
-        act(remote(fr, v.f.at[s, t], v.f_down.at[s], v.f_recv.at[s], me - across, t))
-        act(remote(co, v.c.at[s], v.c_down.at[s], v.c_recv.at[s], me - across, t))
+    def along(act, s, zs, fr, co):
+        up = jnp.logical_and(zs <= z, z < deep - 1)
+        down = jnp.logical_and(zs >= z, z > 0)
+        if fr is not None:
+            pl.when(up)(
+                lambda: act(
+                    remote(fr, v.f.at[s, t], v.f_up.at[s], v.f_recv.at[s], me + across, t)
+                )
+            )
+            pl.when(down)(
+                lambda: act(
+                    remote(fr, v.f.at[s, t], v.f_down.at[s], v.f_recv.at[s], me - across, t)
+                )
+            )
+        if co is not None:
+            pl.when(up)(
+                lambda: act(remote(co, v.c.at[s], v.c_up.at[s], v.c_recv.at[s], me + across, t))
+            )
+            pl.when(down)(
+                lambda: act(remote(co, v.c.at[s], v.c_down.at[s], v.c_recv.at[s], me - across, t))
+            )
 
     def side_frames(act, s, fr):
         for j in range(1, across):
@@ -97,31 +118,80 @@
                 )
             )
 
-    def tile_frames(act, s, fr):
-        for j in range(1, cores):
-            act(
-                remote(
-                    fr, v.f.at[s, t], v.mate_send.at[j - 1, s], v.ft_recv.at[s, t],
-                    me, y * cores + (core + j) % cores,
-                )
-            )
+    def near_rows(act, s, fr):
+        pl.when(has_below)(
+            lambda: act(
+                remote(fr, v.f.at[s, t], v.near_send.at[0, s], v.ft_recv.at[s, t], me, t + 1)
+            )
+        )
+        pl.when(has_above)(
+            lambda: act(
+                remote(fr, v.f.at[s, t], v.near_send.at[1, s], v.ft_recv.at[s, t], me, t - 1)
+            )
+        )
+
+    def far_rows(act, s):
         for j in range(1, high):
-            act(
-                remote(
-                    fr, v.f.at[s, t], v.far_tile.at[j - 1, s], v.ft_recv.at[s, t],
-                    me, (y + j) % high * cores + core,
-                )
-            )
-
-    def pass_on(act, s, j):
-        tt = (y + j) % high * cores + core
-        for i in range(1, cores):
-            act(
-                remote(
-                    v.f.at[s, tt], v.f.at[s, tt], v.pass_send.at[j - 1, i - 1, s],
-                    v.ft_recv.at[s, tt], me, y * cores + (core + i) % cores,
-                )
-            )
+            yy = (y + j) % high
+            beside = jnp.logical_or(
+                jnp.logical_and(yy == y + 1, core == cores - 1),
+                jnp.logical_and(yy == y - 1, core == 0),
+            )
+            pl.when(jnp.logical_not(beside))(
+                lambda j=j, yy=yy: act(
+                    remote(
+                        v.f.at[s, t], v.f.at[s, t], v.far_send.at[j - 1, s], v.ft_recv.at[s, t],
+                        me, yy * cores + core,
+                    )
+                )
+            )
+
+    def entering(body):
+        for j in range(1, high):
+            yy = (y + j) % high
+            for c in range(cores):
+                across_low = jnp.logical_and(yy == y - 1, c == cores - 1)
+                across_high = jnp.logical_and(yy == y + 1, c == 0)
+                straight = jnp.logical_not(jnp.logical_or(across_low, across_high))
+                enters = jnp.logical_or(
+                    jnp.logical_and(across_low, core == 0),
+                    jnp.logical_or(
+                        jnp.logical_and(across_high, core == cores - 1),
+                        jnp.logical_and(straight, core == c),
+                    ),
+                )
+                body(j, c, yy * cores + c, enters, straight)
+
+    def pass_on(act, s):
+        def one(j, c, tt, enters, straight):
+            @pl.when(enters)
+            def _():
+                for i in range(1, cores):
+                    act(
+                        remote(
+                            v.f.at[s, tt], v.f.at[s, tt], v.pass_send.at[j - 1, c, i - 1, s],
+                            v.ft_recv.at[s, tt], me, y * cores + (core + i) % cores,
+                        )
+                    )
+
+        entering(one)
+
+    def gather_far(s):
+        def one(j, c, tt, enters, straight):
+            pl.when(jnp.logical_and(enters, straight))(
+                lambda: received(v.f.at[s, tt], v.ft_recv.at[s, tt])
+            )
+
+        entering(one)
+        pass_on(go, s)
+
+    def gather_passed(s):
+        def one(j, c, tt, enters, straight):
+            pl.when(jnp.logical_not(enters))(
+                lambda: received(v.f.at[s, tt], v.ft_recv.at[s, tt])
+            )
+
+        entering(one)
 
     def edge_down(act, s):
         act(
@@ -200,12 +270,43 @@
     own_notes.start()
     own_weights = pltpu.make_async_copy(weight_ref.at[me], v.w.at[me], v.local_sem.at[2])
     own_weights.start()
-    own_rows = pltpu.make_async_copy(frames_ref, v.f.at[me, t], v.local_sem.at[3])
-    own_rows.start()
-    pl.when(z < deep - 1)(lambda: lift(go, me, frames_ref, cot_ref))
-    pl.when(z > 0)(lambda: sink(go, me, frames_ref, cot_ref))
-    side_frames(go, me, frames_ref)
-    tile_frames(go, me, frames_ref)
+    own_rows.wait()
+    along(go, me, z, v.f.at[me, t], None)
+    side_frames(go, me, v.f.at[me, t])
+    near_rows(go, me, v.f.at[me, t])
+    own_cot.wait()
+    along(go, me, z, None, v.c.at[me])
+
+    def places(s, xo):
+        return [v.ns[s, xo, 0, 1 + c] for c in range(cap)]
+
+    def tile_places(tt, s):
+        return [v.ts[tt, s, x, 0, 1 + c] for c in range(cap)]
+
+    def picked(spots, load):
+        parts = []
+        for c in range(cap):
+            value = jnp.zeros((columns, channels), bf16)
+            for f in range(frames):
+                value = jnp.where(spots[c] == f, load(f), value)
+            parts.append(value)
+        return parts
+
+    def pack(s, zs, load, spots_of):
+        for j in range(1, across):
+            parts = picked(spots_of((x + j) % across), load)
+            for c in range(cap):
+                v.cpo[j - 1, zs, c] = parts[c]
+        side_packed(go, s, zs)
+        parts = picked(spots_of(x), load)
+        for c in range(cap):
+            v.cp[s, c] = parts[c]
+
+    own_scalars.wait()
+    pack(
+        me, z, lambda f: v.c[me, f],
+        lambda xo: [v.os[z * across + xo, 0, 1 + c] for c in range(cap)],
+    )
 
     @pl.when(jnp.logical_not(has_above))
     def _():
@@ -214,6 +315,18 @@
     @pl.when(jnp.logical_not(has_below))
     def _():
         v.below[...] = jnp.zeros_like(v.below)
+
+    @pl.loop(0, experts)
+    def _(k):
+        grad_ref[k] = jnp.zeros_like(grad_ref[k])
+
+    def tile_notes(act):
+        for j in range(1, tiles):
+            act(
+                remote(
+                    v.n, v.tn.at[t], v.tn_send.at[j - 1], v.tn_recv.at[t], me, (t + j) % tiles
+                )
+            )
 
     own_notes.wait()
     own_weights.wait()
@@ -221,15 +334,6 @@
         s = (me + j) % owners
         received(v.n.at[s], v.note_recv.at[0, s])
         received(v.w.at[s], v.note_recv.at[1, s])
-
-    def tile_notes(act):
-        for j in range(1, tiles):
-            act(
-                remote(
-                    v.n, v.tn.at[t], v.tn_send.at[j - 1], v.tn_recv.at[t], me, (t + j) % tiles
-                )
-            )
-
     tile_notes(go)
     copies = [
         pltpu.make_async_copy(v.n, v.tn.at[t], v.local_sem.at[1]),
@@ -241,51 +345,28 @@
     for copy in copies:
         copy.wait()
 
-    def places(s, xo):
-        return [v.ns[s, xo, 0, 1 + c] for c in range(cap)]
-
-    def tile_places(tt, s):
-        return [v.ts[tt, s, x, 0, 1 + c] for c in range(cap)]
-
-    def picked(spots, load):
-        parts = []
-        for c in range(cap):
-            value = jnp.zeros((columns, channels), bf16)
-            for f in range(frames):
-                value = jnp.where(spots[c] == f, load(f), value)
-            parts.append(value)
-        return parts
-
-    def pack(s, zs, load):
-        for j in range(1, across):
-            parts = picked(places(s, (x + j) % across), load)
-            for c in range(cap):
-                v.cpo[j - 1, zs, c] = parts[c]
-        parts = picked(places(s, x), load)
-        for c in range(cap):
-            v.cp[s, c] = parts[c]
-        side_packed(go, s, zs)
-
-    pack(me, z, lambda f: cot_ref[f])
-
-    for j in range(1, tiles):
-        tt = (t + j) % tiles
-        received(v.tn.at[tt], v.tn_recv.at[tt])
-    tile_scalars = pltpu.make_async_copy(v.tn, v.ts, v.local_sem.at[1])
-    tile_scalars.start()
-    tile_scalars.wait()
-    own_rows.wait()
-    load_bank.wait()
-
-    count = (2 * deep - 1) * across
+    def settle():
+        for j in range(1, tiles):
+            tt = (t + j) % tiles
+            received(v.tn.at[tt], v.tn_recv.at[tt])
+        tile_scalars = pltpu.make_async_copy(v.tn, v.ts, v.local_sem.at[1])
+        tile_scalars.start()
+        tile_scalars.wait()
+        load_bank.wait()
+
+    step = 2 * across
+    count = (deep + 1) * step
 
     def stage(n, body, lead=None):
-        j, xj = n // across, n % across
-        zs = z + (j + 1) // 2 * (1 - 2 * (j % 2))
+        k, sign, xj = n // step, n % 2, n % step // 2
+        hops = k - (xj + across - 1) // across
+        zs = z + hops * (2 * sign - 1)
         s = zs * across + (x + xj) % across
         cond = jnp.logical_and(
             jnp.logical_and(n >= 0, n < count), jnp.logical_and(zs >= 0, zs < deep)
         )
+        cond = jnp.logical_and(cond, jnp.logical_and(hops >= 0, hops + 1 - sign > 0))
+        cond = jnp.logical_and(cond, hops < deep)
         if lead is True:
             cond = jnp.logical_and(cond, xj == 0)
         elif lead is False:
@@ -297,28 +378,21 @@
 
         @pl.when(xj == 0)
         def _():
+            along(go, s, zs, v.f.at[s, t], None)
+            side_frames(go, s, v.f.at[s, t])
+
+        near_rows(go, s, v.f.at[s, t])
+
+        @pl.when(xj == 0)
+        def _():
             received(v.c.at[s], v.c_recv.at[s])
-            pl.when(jnp.logical_and(zs < z, z < deep - 1))(
-                lambda: lift(go, s, v.f.at[s, t], v.c.at[s])
-            )
-            pl.when(jnp.logical_and(zs > z, z > 0))(
-                lambda: sink(go, s, v.f.at[s, t], v.c.at[s])
-            )
-            side_frames(go, s, v.f.at[s, t])
-            pack(s, zs, lambda f: v.c[s, f])
+            along(go, s, zs, None, v.c.at[s])
+            pack(s, zs, lambda f: v.c[s, f], lambda xo: places(s, xo))
 
         @pl.when(xj > 0)
         def _():
             received(v.cp.at[s], v.cp_recv.at[s])
 
-        tile_frames(go, s, v.f.at[s, t])
-
-    def across_tiles(s, zs, xj):
-        for j in range(1, high):
-            tt = (y + j) % high * cores + core
-            received(v.f.at[s, tt], v.ft_recv.at[s, tt])
-            pass_on(go, s, j)
-
     place = lax.broadcasted_iota(jnp.int32, (rows, 1), 0)
     item = place // columns
     column = place % columns
@@ -330,10 +404,8 @@
         return jnp.where(column == columns - 1, 0.0, pltpu.roll(value, rows - 1, 0))
 
     def compute(s, zs, xj):
-        for j in range(high):
-            for i in range(1, cores):
-                tt = (y + j) % high * cores + (core + i) % cores
-                received(v.f.at[s, tt], v.ft_recv.at[s, tt])
+        pl.when(has_above)(lambda: received(v.f.at[s, t_above], v.ft_recv.at[s, t_above]))
+        pl.when(has_below)(lambda: received(v.f.at[s, t_below], v.ft_recv.at[s, t_below]))
         e = v.ns[s, x, 0, 0]
         spots = places(s, x)
         blank = jnp.zeros((rows, channels), bf16)
@@ -453,31 +525,18 @@
         @pl.when(zs == z)
         def _():
             for f in range(frames):
-                v.base[0, f] = v.total[0, f] + cot_ref[f].astype(f32)
-                v.base[1, f] = v.total[1, f] + frames_ref[f].astype(f32)
+                v.base[0, f] = v.total[0, f] + v.c[me, f].astype(f32)
+                v.base[1, f] = v.total[1, f] + v.f[me, t, f].astype(f32)
 
         @pl.when(zs != z)
         def _():
             v.fo[zs] = v.total[...].astype(bf16)
             far_terms(go, zs)
 
-    @pl.loop(0, count + across + 3)
-    def _(n):
-        stage(n - 2, compute)
-        stage(n - 3, to_side, lead=False)
-        stage(n - across - 3, to_far, lead=True)
-        stage(n - 1, across_tiles)
-        pl.when(n > 0)(lambda: stage(n, arrive))
-
-    @pl.loop(0, experts)
-    def _(k):
-        grad_ref[k] = jnp.zeros_like(grad_ref[k])
-
     lane = lax.broadcasted_iota(jnp.int32, (1, rows), 1) % columns
 
-    @pl.loop(0, owners)
-    def _(i):
-        s = (me + i) % owners
+    def weigh(s, zs, xj):
+        gather_passed(s)
         for j in range(1, tiles):
             tt = (t + j) % tiles
             received(v.gi.at[s, tt], v.g_recv.at[s, tt])
@@ -508,6 +567,17 @@
                 term = jnp.dot(v.gt[db], v.xw[da], preferred_element_type=f32)
                 grad_ref[:, 3 * da + db] += term.reshape(experts, share, channels)
 
+    @pl.loop(0, count + (count + 2 * step))
+    def _(n):
+        pl.when(n == step)(settle)
+        stage(n - step, compute)
+        stage(n - 2 * step, to_side, lead=False)
+        stage(n - (count + step), lambda s, zs, xj: gather_far(s))
+        stage(n - (4 * step + 2), to_far, lead=True)
+        stage(n - (count + 2 * step), weigh)
+        stage(n - count, lambda s, zs, xj: far_rows(go, s))
+        pl.when(n > 1)(lambda: stage(n, arrive))
+
     for k in range(1, deep):
         zs = (z + k) % deep
         received(v.fi.at[zs], v.fi_recv.at[zs])
@@ -526,26 +596,19 @@
         gates(drain, s)
     send_notes(drain)
     tile_notes(drain)
-    pl.when(z < deep - 1)(lambda: lift(drain, me, frames_ref, cot_ref))
-    pl.when(z > 0)(lambda: sink(drain, me, frames_ref, cot_ref))
 
     def finish(s, zs, xj):
         @pl.when(xj == 0)
         def _():
-            pl.when(jnp.logical_and(zs < z, z < deep - 1))(
-                lambda: lift(drain, s, v.f.at[s, t], v.c.at[s])
-            )
-            pl.when(jnp.logical_and(zs > z, z > 0))(
-                lambda: sink(drain, s, v.f.at[s, t], v.c.at[s])
-            )
+            along(drain, s, zs, v.f.at[s, t], v.c.at[s])
             side_frames(drain, s, v.f.at[s, t])
             side_packed(drain, s, zs)
             pl.when(zs != z)(lambda: far_terms(drain, zs))
 
         pl.when(xj > 0)(lambda: side_terms(drain, s, zs, xj))
-        tile_frames(drain, s, v.f.at[s, t])
-        for j in range(1, high):
-            pass_on(drain, s, j)
+        near_rows(drain, s, v.f.at[s, t])
+        far_rows(drain, s)
+        pass_on(drain, s)
         slices(drain, s)
         pl.when(has_above)(lambda: edge_up(drain, s))
         pl.when(has_below)(lambda: edge_down(drain, s))
@@ -565,7 +628,7 @@
     cap = CAP
     rows = cap * columns
     dma = pltpu.SemaphoreType.DMA
-    vmem = pl.BlockSpec(memory_space=pltpu.VMEM)
+    vmem, hbm = pl.BlockSpec(memory_space=pltpu.VMEM), pl.BlockSpec(memory_space=pltpu.HBM)
     bf16, f32, i32 = jnp.bfloat16, jnp.float32, jnp.int32
     beside, mates, far = (max(value - 1, 1) for value in (across, cores, high))
     others, peers = max(owners - 1, 1), max(tiles - 1, 1)
@@ -577,6 +640,7 @@
         n=pltpu.VMEM((owners, across, 1, 128), i32),
         w=pltpu.VMEM((owners, 1, 128), f32),
         tn=pltpu.VMEM((tiles, owners, across, 1, 128), i32),
+        os=pltpu.SMEM((owners, 1, 128), i32),
         ns=pltpu.SMEM((owners, across, 1, 128), i32),
         ws=pltpu.SMEM((owners, 1, 128), f32),
         ts=pltpu.SMEM((tiles, owners, across, 1, 128), i32),
@@ -598,15 +662,15 @@
         base=pltpu.VMEM((2, count, columns, channels), f32),
         xw=pltpu.VMEM((3, tiles * rows, channels), bf16),
         gt=pltpu.VMEM((3, experts * share, tiles * rows), bf16),
-        local_sem=dma((5,)),
+        local_sem=dma((6,)),
         spare_sem=dma((1,)),
         note_send=dma((2, others)), note_recv=dma((2, owners)),
         tn_send=dma((peers,)), tn_recv=dma((tiles,)),
         f_up=dma((owners,)), f_down=dma((owners,)), f_side=dma((beside, owners)), f_recv=dma((owners,)),
         c_up=dma((owners,)), c_down=dma((owners,)), c_recv=dma((owners,)),
         cp_send=dma((beside, deep)), cp_recv=dma((owners,)),
-        mate_send=dma((mates, owners)), far_tile=dma((far, owners)),
-        pass_send=dma((far, mates, owners)), ft_recv=dma((owners, tiles)),
+        near_send=dma((2, owners)), far_send=dma((far, owners)),
+        pass_send=dma((far, cores, mates, owners)), ft_recv=dma((owners, tiles)),
         above_send=dma((owners,)), above_recv=dma((owners,)),
         below_send=dma((owners,)), below_recv=dma((owners,)),
         g_send=dma((peers, owners)), g_recv=dma((owners, tiles)),
@@ -615,6 +679,10 @@
         sa_send=dma((beside, deep)), sa_recv=dma((beside, deep)),
         fo_send=dma((deep,)), fi_recv=dma((deep,)),
     )
+    held = 2 * frames.size * 4 * 2 + experts * taps * share * channels * 4 + owners * 8 * 128 * 4
+    for ref in scratch.values():
+        if ref.memory_space == pltpu.VMEM:
+            held += math.prod(ref.shape) * jnp.dtype(ref.dtype).itemsize
     return pl.pallas_call(
         functools.partial(layer_kernel, deep, across, high, cores, tuple(scratch)),
         out_shape=[
@@ -623,14 +691,15 @@
             jax.ShapeDtypeStruct((owners, 8, 128), f32),
             jax.ShapeDtypeStruct((experts, taps, share, channels), f32),
         ],
-        in_specs=[vmem] * 4 + [pl.BlockSpec(memory_space=pl.ANY)],
+        in_specs=[hbm, hbm, vmem, vmem, hbm],
         out_specs=[vmem] * 4,
         scratch_shapes=list(scratch.values()),
         compiler_params=pltpu.CompilerParams(
-            collective_id=0, has_side_effects=True, vmem_limit_bytes=58 * 1024 * 1024
+            collective_id=0, has_side_effects=True, vmem_limit_bytes=held + (8 << 20)
         ),
         name="layer",
-    )(frames, cot, note, weight, kernels)
+    )(*(pltpu.with_memory_space_constraint(v, pltpu.HBM) for v in (frames, cot)), note, weight,
+      pltpu.with_memory_space_constraint(kernels, pltpu.HBM))
 
 
 def shards(frames, kernels, experts, counts, gate_weights, cotangent):

time: 110 us -> 77.5 us (0.70)
  the two profiles are of different devices: /device:TPU:1 before, /device:TPU:0 now
where the time goes in v2:
time: 77.5 us; the launch traced here: 76.9 us
  Pallas kernels  70.1 us (90%)
  other arithmetic  3.17 us (4%)
  local copies, waits for them, and re-layouts  2.99 us (4%)
    pallas_call x1, Pallas kernels, layer(): pl.pallas_call(functools.partial(layer_kernel, deep, across, high, cores,...  70.1 us
    unnamed x3, local copies, waits for them, and re-layouts  2.71 us

profile of v2, /device:TPU:0, one launch (start us, length us, event | category | flops | bytes accessed | tf_op | source)
XLA Modules:
  0.0 76.9 jit_solution(13707823357197180484)
XLA Ops:
  0.6 0.7 iota_compare_fusion.2
  1.4 0.7 add_select_fusion
  2.1 0.8 %select_reduce_fusion.1 = (f32[4,8]{1,0:T(4,128)S(1)}, pred[4,4,8]{2,1,0:T(4,128)(4,1)S(1)}) fusion(f32[4,4]{1,0:T(4,128)} %bitcast.36, pred[4,4]{1,0:T(4,128)(4,1)S(1)} %iota_compare_fusion.2, s32[4,4]{1,0:T(4,128)S(1)} %get-tuple-element.25), kind=kLoop, calls=%fused_computation.1 | loop fusion | flops 480 | bytes 400 | tf_op jit(solution)/shard_map/reduce_sum | solution.py:720
  2.8 0.1 select_reduce_fusion.2
  3.0 0.1 select_reduce_fusion.5
  3.1 0.1 copy.19
  3.2 0.1 copy.20
  3.3 70.1 %layer.1 = (bf16[4,64,256]{2,1,0:T(8,128)(2,1)S(1)}, bf16[4,64,256]{2,1,0:T(8,128)(2,1)S(1)}, f32[8,8,128]{2,1,0:T(8,128)S(1)}, f32[4,9,64,256]{3,2,1,0:T(8,128)S(1)}) custom-call(bf16[4,64,256]{2,1,0:T(8,128)(2,1)} %bitcast.28, bf16[4,64,256]{2,1,0:T(8,128)(2,1)} %bitcast.29, s32[8,1,128]{2,1,0:T(1,128)S(1)} %pad.8.note_ref, ...), custom_call_target="tpu_custom_call" | custom-call | tf_op jit(solution)/shard_map/layer/pallas_call | solution.py:686
  73.4 0.1 copy.21
  73.5 0.7 select_reduce_fusion
  74.2 0.7 copy.28
  74.8 0.7 copy.29
  75.5 1.4 %copy.30 = f32[4,9,256,64]{2,3,1,0:T(8,128)} copy(f32[4,9,256,64]{2,3,1,0:T(8,128)S(1)} %bitcast.25) | data formatting | bytes 4718592
  (12 shorter events, 0.2 us)

commit v3 on v2

--- a/solution.py
+++ b/solution.py
@@ -47,15 +47,15 @@
 ):
     v = SimpleNamespace(**dict(zip(names, rest)))
     me, t = lax.axis_index("dp"), lax.axis_index("tile")
-    z, x = me // across, me % across
-    y, core = t // cores, t % cores
+    z, x = lax.div(me, across), lax.rem(me, across)
+    y, core = lax.div(t, cores), lax.rem(t, cores)
     owners, tiles = deep * across, high * cores
     _, _, frames, columns, channels = v.f.shape
     experts, taps, share, _ = grad_ref.shape
     cap = CAP
     rows = cap * columns
     has_above, has_below = t > 0, t < tiles - 1
-    t_above, t_below = (t + tiles - 1) % tiles, (t + 1) % tiles
+    t_above, t_below = lax.rem(t + tiles - 1, tiles), lax.rem(t + 1, tiles)
     bf16, f32 = jnp.bfloat16, jnp.float32
 
     load_bank = pltpu.make_async_copy(bank_hbm, v.bank, v.local_sem.at[0])
@@ -70,11 +70,11 @@
     barrier = pltpu.get_barrier_semaphore()
     for j in range(1, owners):
         pl.semaphore_signal(
-            barrier, device_id=((me + j) % owners, t), device_id_type=pl.DeviceIdType.MESH
+            barrier, device_id=(lax.rem(me + j, owners), t), device_id_type=pl.DeviceIdType.MESH
         )
     for j in range(1, tiles):
         pl.semaphore_signal(
-            barrier, device_id=(me, (t + j) % tiles), device_id_type=pl.DeviceIdType.MESH
+            barrier, device_id=(me, lax.rem(t + j, tiles)), device_id_type=pl.DeviceIdType.MESH
         )
     pl.semaphore_wait(barrier, owners - 1 + tiles - 1)
 
@@ -84,28 +84,28 @@
         if fr is not None:
             pl.when(up)(
                 lambda: act(
-                    remote(fr, v.f.at[s, t], v.f_up.at[s], v.f_recv.at[s], me + across, t)
+                    remote(fr, v.f.at[s, t], v.f_up.at[zs], v.f_recv.at[s], me + across, t)
                 )
             )
             pl.when(down)(
                 lambda: act(
-                    remote(fr, v.f.at[s, t], v.f_down.at[s], v.f_recv.at[s], me - across, t)
+                    remote(fr, v.f.at[s, t], v.f_down.at[zs], v.f_recv.at[s], me - across, t)
                 )
             )
         if co is not None:
             pl.when(up)(
-                lambda: act(remote(co, v.c.at[s], v.c_up.at[s], v.c_recv.at[s], me + across, t))
+                lambda: act(remote(co, v.c.at[s], v.c_up.at[zs], v.c_recv.at[zs], me + across, t))
             )
             pl.when(down)(
-                lambda: act(remote(co, v.c.at[s], v.c_down.at[s], v.c_recv.at[s], me - across, t))
-            )
-
-    def side_frames(act, s, fr):
+                lambda: act(remote(co, v.c.at[s], v.c_down.at[zs], v.c_recv.at[zs], me - across, t))
+            )
+
+    def side_frames(act, s, zs, fr):
         for j in range(1, across):
             act(
                 remote(
-                    fr, v.f.at[s, t], v.f_side.at[j - 1, s], v.f_recv.at[s],
-                    z * across + (x + j) % across, t,
+                    fr, v.f.at[s, t], v.f_side.at[j - 1, zs], v.f_recv.at[s],
+                    z * across + lax.rem(x + j, across), t,
                 )
             )
 
@@ -114,7 +114,7 @@
             act(
                 remote(
                     v.cpo.at[j - 1, zs], v.cp.at[s], v.cp_send.at[j - 1, zs], v.cp_recv.at[s],
-                    z * across + (x + j) % across, t,
+                    z * across + lax.rem(x + j, across), t,
                 )
             )
 
@@ -132,7 +132,7 @@
 
     def far_rows(act, s):
         for j in range(1, high):
-            yy = (y + j) % high
+            yy = lax.rem(y + j, high)
             beside = jnp.logical_or(
                 jnp.logical_and(yy == y + 1, core == cores - 1),
                 jnp.logical_and(yy == y - 1, core == 0),
@@ -148,7 +148,7 @@
 
     def entering(body):
         for j in range(1, high):
-            yy = (y + j) % high
+            yy = lax.rem(y + j, high)
             for c in range(cores):
                 across_low = jnp.logical_and(yy == y - 1, c == cores - 1)
                 across_high = jnp.logical_and(yy == y + 1, c == 0)
@@ -170,7 +170,7 @@
                     act(
                         remote(
                             v.f.at[s, tt], v.f.at[s, tt], v.pass_send.at[j - 1, c, i - 1, s],
-                            v.ft_recv.at[s, tt], me, y * cores + (core + i) % cores,
+                            v.ft_recv.at[s, tt], me, y * cores + lax.rem(core + i, cores),
                         )
                     )
 
@@ -207,63 +207,63 @@
             )
         )
 
-    def slices(act, s):
+    def slices(s):
         for j in range(1, tiles):
-            tt = (t + j) % tiles
-            act(
-                remote(
-                    v.go.at[s, tt], v.gi.at[s, t], v.g_send.at[j - 1, s], v.g_recv.at[s, t], me, tt
-                )
-            )
-
-    def gates(act, s):
+            tt = lax.rem(t + j, tiles)
+            go(remote(v.go.at[s, tt], v.gi.at[s, t], v.g_send.at[s], v.g_recv.at[s], me, tt))
+
+    def gates(s):
+        go(remote(v.gate.at[s], gated_ref.at[me], v.gate_send.at[0], v.gate_recv.at[0], s, t))
+
+    def side_act(act, s, zs, xj):
         act(
             remote(
-                v.gate.at[s], gated_ref.at[me], v.gate_send.at[s], v.gate_recv.at[me], s, t
-            )
-        )
-
-    def side_terms(act, s, zs, xj):
+                v.act.at[s], v.sai.at[xj - 1, zs],
+                v.sa_send.at[xj - 1, zs], v.sa_recv.at[xj - 1, zs],
+                z * across + lax.rem(s, across), t,
+            )
+        )
+
+    def side_back(act, s, zs, xj):
         act(
             remote(
                 v.sbo.at[xj - 1, zs], v.sbi.at[xj - 1, zs],
-                v.sb_send.at[xj - 1, zs], v.sb_recv.at[xj - 1, zs], z * across + s % across, t,
-            )
-        )
+                v.sb_send.at[xj - 1, zs], v.sb_recv.at[xj - 1, zs],
+                z * across + lax.rem(s, across), t,
+            )
+        )
+
+    def far_terms(act, zs, part):
         act(
             remote(
-                v.act.at[s], v.sai.at[xj - 1, zs],
-                v.sa_send.at[xj - 1, zs], v.sa_recv.at[xj - 1, zs], z * across + s % across, t,
-            )
-        )
-
-    def far_terms(act, zs):
-        act(
-            remote(
-                v.fo.at[zs], v.fi.at[z], v.fo_send.at[zs], v.fi_recv.at[z], zs * across + x, t
-            )
-        )
+                v.fo.at[zs, part], v.fi.at[z, part],
+                v.fo_send.at[part, zs], v.fi_recv.at[part, z], zs * across + x, t,
+            )
+        )
+
+    def sent(ref, sem):
+        remote(ref, ref, sem, v.spare_sem.at[0], me, t).wait_send()
 
     def received(ref, sem):
         remote(ref, ref, v.spare_sem.at[0], sem, me, t).wait_recv()
 
-    def send_notes(act):
+    def send_notes():
         for j in range(1, owners):
-            peer = (me + j) % owners
-            act(
+            peer = lax.rem(me + j, owners)
+            go(
                 remote(
-                    note_ref.at[pl.ds(peer // across * across, across)], v.n.at[me],
-                    v.note_send.at[0, j - 1], v.note_recv.at[0, me], peer, t,
-                )
-            )
-            act(
+                    note_ref.at[pl.ds(lax.div(peer, across) * across, across)], v.n.at[me],
+                    v.note_send.at[0], v.note_recv.at[0], peer, t,
+                )
+            )
+            go(
                 remote(
                     weight_ref.at[peer], v.w.at[me],
-                    v.note_send.at[1, j - 1], v.note_recv.at[1, me], peer, t,
-                )
-            )
-
-    send_notes(go)
+                    v.note_send.at[1], v.note_recv.at[1], peer, t,
+                )
+            )
+
+    send_notes()
     own_notes = pltpu.make_async_copy(
         note_ref.at[pl.ds(z * across, across)], v.n.at[me], v.local_sem.at[1]
     )
@@ -272,7 +272,7 @@
     own_weights.start()
     own_rows.wait()
     along(go, me, z, v.f.at[me, t], None)
-    side_frames(go, me, v.f.at[me, t])
+    side_frames(go, me, z, v.f.at[me, t])
     near_rows(go, me, v.f.at[me, t])
     own_cot.wait()
     along(go, me, z, None, v.c.at[me])
@@ -294,7 +294,7 @@
 
     def pack(s, zs, load, spots_of):
         for j in range(1, across):
-            parts = picked(spots_of((x + j) % across), load)
+            parts = picked(spots_of(lax.rem(x + j, across)), load)
             for c in range(cap):
                 v.cpo[j - 1, zs, c] = parts[c]
         side_packed(go, s, zs)
@@ -320,21 +320,15 @@
     def _(k):
         grad_ref[k] = jnp.zeros_like(grad_ref[k])
 
-    def tile_notes(act):
+    def tile_notes():
         for j in range(1, tiles):
-            act(
-                remote(
-                    v.n, v.tn.at[t], v.tn_send.at[j - 1], v.tn_recv.at[t], me, (t + j) % tiles
-                )
-            )
+            go(remote(v.n, v.tn.at[t], v.tn_send.at[0], v.tn_recv.at[0], me, lax.rem(t + j, tiles)))
 
     own_notes.wait()
     own_weights.wait()
-    for j in range(1, owners):
-        s = (me + j) % owners
-        received(v.n.at[s], v.note_recv.at[0, s])
-        received(v.w.at[s], v.note_recv.at[1, s])
-    tile_notes(go)
+    received(v.n.at[pl.ds(0, owners - 1)], v.note_recv.at[0])
+    received(v.w.at[pl.ds(0, owners - 1)], v.note_recv.at[1])
+    tile_notes()
     copies = [
         pltpu.make_async_copy(v.n, v.tn.at[t], v.local_sem.at[1]),
         pltpu.make_async_copy(v.n, v.ns, v.local_sem.at[2]),
@@ -346,29 +340,27 @@
         copy.wait()
 
     def settle():
-        for j in range(1, tiles):
-            tt = (t + j) % tiles
-            received(v.tn.at[tt], v.tn_recv.at[tt])
+        received(v.tn.at[pl.ds(0, tiles - 1)], v.tn_recv.at[0])
         tile_scalars = pltpu.make_async_copy(v.tn, v.ts, v.local_sem.at[1])
         tile_scalars.start()
         tile_scalars.wait()
-        load_bank.wait()
 
     step = 2 * across
     count = (deep + 1) * step
 
     def stage(n, body, lead=None):
-        k, sign, xj = n // step, n % 2, n % step // 2
-        hops = k - (xj + across - 1) // across
+        k, slot = lax.div(n, step), lax.rem(n, step)
+        sign, xj = lax.rem(slot, 2), lax.div(slot, 2)
+        hops = k - lax.div(xj + across - 1, across)
         zs = z + hops * (2 * sign - 1)
-        s = zs * across + (x + xj) % across
+        s = zs * across + lax.rem(x + xj, across)
         cond = jnp.logical_and(
             jnp.logical_and(n >= 0, n < count), jnp.logical_and(zs >= 0, zs < deep)
         )
         cond = jnp.logical_and(cond, jnp.logical_and(hops >= 0, hops + 1 - sign > 0))
         cond = jnp.logical_and(cond, hops < deep)
         if lead is True:
-            cond = jnp.logical_and(cond, xj == 0)
+            cond = jnp.logical_and(cond, jnp.logical_and(xj == 0, n > 0))
         elif lead is False:
             cond = jnp.logical_and(cond, xj > 0)
         pl.when(cond)(lambda: body(s, zs, xj))
@@ -379,13 +371,13 @@
         @pl.when(xj == 0)
         def _():
             along(go, s, zs, v.f.at[s, t], None)
-            side_frames(go, s, v.f.at[s, t])
+            side_frames(go, s, zs, v.f.at[s, t])
 
         near_rows(go, s, v.f.at[s, t])
 
         @pl.when(xj == 0)
         def _():
-            received(v.c.at[s], v.c_recv.at[s])
+            received(v.c.at[s], v.c_recv.at[zs])
             along(go, s, zs, None, v.c.at[s])
             pack(s, zs, lambda f: v.c[s, f], lambda xo: places(s, xo))
 
@@ -437,6 +429,7 @@
         activated = pre * squash
         slope = squash * (1.0 + pre * (1.0 - squash))
         v.act[s] = (weight * activated).astype(bf16).reshape(cap, columns, channels)
+        pl.when(xj > 0)(lambda: side_act(go, s, zs, xj))
         sums = jnp.sum((upstream * activated).reshape(cap, columns, channels), axis=1)
         sums = jnp.broadcast_to(jnp.sum(sums, axis=1, keepdims=True), (cap, 128))
         sums = jnp.concatenate([sums, jnp.zeros((8 - cap, 128), f32)], axis=0)
@@ -444,7 +437,7 @@
 
         @pl.when(s != me)
         def _():
-            gates(go, s)
+            gates(s)
 
         @pl.when(s == me)
         def _():
@@ -455,7 +448,7 @@
         for k in range(tiles):
             v.go[s, k] = turned[k * share : (k + 1) * share]
         v.gi[s, t] = v.go[s, t]
-        slices(go, s)
+        slices(s)
         for da in (0, 2, 1):
             parts = [
                 lax.dot_general(
@@ -480,9 +473,10 @@
         pl.when(has_below)(lambda: received(v.below.at[s], v.below_recv.at[s]))
 
     def spread_out(value, spots, load, f):
+        found = jnp.zeros((columns, channels), bf16)
         for c in range(cap):
-            value = value + jnp.where(spots[c] == f, load(c).astype(f32), 0.0)
-        return value
+            found = jnp.where(spots[c] == f, load(c), found)
+        return value + found.astype(f32)
 
     def back_rows(s):
         mine = places(s, x)
@@ -502,44 +496,58 @@
         row = back_rows(s)
         for f in range(frames):
             v.sbo[xj - 1, zs, f] = row(f).astype(bf16)
-        side_terms(go, s, zs, xj)
-
-    def to_far(s, zs, xj):
+        side_back(go, s, zs, xj)
+
+    def far_act(s, zs, xj):
+        for j in range(1, across):
+            received(v.sai.at[j - 1, zs], v.sa_recv.at[j - 1, zs])
+        spots = [places(s, x)] + [
+            places(s, lax.rem(x + across - j, across)) for j in range(1, across)
+        ]
+        for f in range(frames):
+            value = spread_out(
+                jnp.zeros((columns, channels), f32), spots[0], lambda c: v.act[s, c], f
+            )
+            for j in range(1, across):
+                value = spread_out(value, spots[j], lambda c: v.sai[j - 1, zs, c], f)
+            v.total[1, f] = value
+
+        @pl.when(zs == z)
+        def _():
+            for f in range(frames):
+                v.base[1, f] = v.total[1, f] + v.f[me, t, f].astype(f32)
+
+        @pl.when(zs != z)
+        def _():
+            v.fo[zs, 1] = v.total[1].astype(bf16)
+            far_terms(go, zs, 1)
+
+    def far_back(s, zs, xj):
         rims(s)
         for j in range(1, across):
             received(v.sbi.at[j - 1, zs], v.sb_recv.at[j - 1, zs])
-            received(v.sai.at[j - 1, zs], v.sa_recv.at[j - 1, zs])
         row = back_rows(s)
-        spots = [places(s, x)] + [places(s, (x + across - j) % across) for j in range(1, across)]
         for f in range(frames):
-            first = row(f)
-            second = spread_out(
-                jnp.zeros((columns, channels), f32), spots[0], lambda c: v.act[s, c], f
-            )
+            value = row(f)
             for j in range(1, across):
-                first = first + v.sbi[j - 1, zs, f].astype(f32)
-                second = spread_out(second, spots[j], lambda c: v.sai[j - 1, zs, c], f)
-            v.total[0, f] = first
-            v.total[1, f] = second
+                value = value + v.sbi[j - 1, zs, f].astype(f32)
+            v.total[0, f] = value
 
         @pl.when(zs == z)
         def _():
             for f in range(frames):
                 v.base[0, f] = v.total[0, f] + v.c[me, f].astype(f32)
-                v.base[1, f] = v.total[1, f] + v.f[me, t, f].astype(f32)
 
         @pl.when(zs != z)
         def _():
-            v.fo[zs] = v.total[...].astype(bf16)
-            far_terms(go, zs)
+            v.fo[zs, 0] = v.total[0].astype(bf16)
+            far_terms(go, zs, 0)
 
     lane = lax.broadcasted_iota(jnp.int32, (1, rows), 1) % columns
 
     def weigh(s, zs, xj):
         gather_passed(s)
-        for j in range(1, tiles):
-            tt = (t + j) % tiles
-            received(v.gi.at[s, tt], v.g_recv.at[s, tt])
+        received(v.gi.at[s, pl.ds(0, tiles - 1)], v.g_recv.at[s])
         for tt in range(tiles):
             e = v.ts[tt, s, x, 0, 0]
             spots = tile_places(tt, s)
@@ -567,55 +575,68 @@
                 term = jnp.dot(v.gt[db], v.xw[da], preferred_element_type=f32)
                 grad_ref[:, 3 * da + db] += term.reshape(experts, share, channels)
 
-    @pl.loop(0, count + (count + 2 * step))
+    @pl.loop(0, count + (4 * step + 2))
     def _(n):
-        pl.when(n == step)(settle)
+        pl.when(n == step)(load_bank.wait)
+        pl.when(n == (step + 3))(settle)
         stage(n - step, compute)
-        stage(n - 2 * step, to_side, lead=False)
-        stage(n - (count + step), lambda s, zs, xj: gather_far(s))
-        stage(n - (4 * step + 2), to_far, lead=True)
-        stage(n - (count + 2 * step), weigh)
-        stage(n - count, lambda s, zs, xj: far_rows(go, s))
+        stage(n - (step + 3), to_side, lead=False)
+        stage(n - 4 * step, far_act, lead=True)
+        stage(n - (4 * step + 2), far_back, lead=True)
+        stage(n - (4 * step + 2), lambda s, zs, xj: far_rows(go, s))
         pl.when(n > 1)(lambda: stage(n, arrive))
 
+    @pl.loop(0, count + 2)
+    def _(n):
+        stage(n, lambda s, zs, xj: gather_far(s))
+        stage(n - 2, weigh)
+
+    some = pl.ds(0, owners - 1)
+    received(gated_ref.at[some], v.gate_recv.at[0])
+    sent(v.gate.at[some], v.gate_send.at[0])
+    sent(v.n.at[some], v.note_send.at[0])
+    sent(v.w.at[some], v.note_send.at[1])
+    sent(v.tn.at[pl.ds(0, tiles - 1)], v.tn_send.at[0])
+
+    def finish(s, zs, xj):
+        @pl.when(xj == 0)
+        def _():
+            along(drain, s, zs, v.f.at[s, t], v.c.at[s])
+            side_frames(drain, s, zs, v.f.at[s, t])
+            side_packed(drain, s, zs)
+            for part in range(2):
+                pl.when(zs != z)(lambda part=part: far_terms(drain, zs, part))
+
+        @pl.when(xj > 0)
+        def _():
+            side_act(drain, s, zs, xj)
+            side_back(drain, s, zs, xj)
+
+        near_rows(drain, s, v.f.at[s, t])
+        far_rows(drain, s)
+        pass_on(drain, s)
+        sent(v.go.at[s, pl.ds(0, tiles - 1)], v.g_send.at[s])
+        pl.when(has_above)(lambda: edge_up(drain, s))
+        pl.when(has_below)(lambda: edge_down(drain, s))
+
+    @pl.loop(0, count)
+    def _(n):
+        stage(n, finish)
+
+    far_act(me, z, 0)
+    far_back(me, z, 0)
     for k in range(1, deep):
-        zs = (z + k) % deep
-        received(v.fi.at[zs], v.fi_recv.at[zs])
+        zs = lax.rem(z + k, deep)
+        for part in range(2):
+            received(v.fi.at[zs, part], v.fi_recv.at[part, zs])
     for f in range(frames):
         first, second = v.base[0, f], v.base[1, f]
         for k in range(1, deep):
-            zs = (z + k) % deep
+            zs = lax.rem(z + k, deep)
             first = first + v.fi[zs, 0, f].astype(f32)
             second = second + v.fi[zs, 1, f].astype(f32)
         input_ref[f] = first.astype(bf16)
         result_ref[f] = second.astype(bf16)
-
-    for j in range(1, owners):
-        s = (me + j) % owners
-        received(gated_ref.at[s], v.gate_recv.at[s])
-        gates(drain, s)
-    send_notes(drain)
-    tile_notes(drain)
-
-    def finish(s, zs, xj):
-        @pl.when(xj == 0)
-        def _():
-            along(drain, s, zs, v.f.at[s, t], v.c.at[s])
-            side_frames(drain, s, v.f.at[s, t])
-            side_packed(drain, s, zs)
-            pl.when(zs != z)(lambda: far_terms(drain, zs))
-
-        pl.when(xj > 0)(lambda: side_terms(drain, s, zs, xj))
-        near_rows(drain, s, v.f.at[s, t])
-        far_rows(drain, s)
-        pass_on(drain, s)
-        slices(drain, s)
-        pl.when(has_above)(lambda: edge_up(drain, s))
-        pl.when(has_below)(lambda: edge_down(drain, s))
-
-    @pl.loop(0, count)
-    def _(n):
-        stage(n, finish)
 
 
 def layer(frames, cot, note, weight, kernels, owners, tiles):
@@ -631,7 +652,6 @@
     vmem, hbm = pl.BlockSpec(memory_space=pltpu.VMEM), pl.BlockSpec(memory_space=pltpu.HBM)
     bf16, f32, i32 = jnp.bfloat16, jnp.float32, jnp.int32
     beside, mates, far = (max(value - 1, 1) for value in (across, cores, high))
-    others, peers = max(owners - 1, 1), max(tiles - 1, 1)
     scratch = dict(
         f=pltpu.VMEM((owners, tiles, count, columns, channels), bf16),
         c=pltpu.VMEM((owners, count, columns, channels), bf16),
@@ -664,20 +684,20 @@
         gt=pltpu.VMEM((3, experts * share, tiles * rows), bf16),
         local_sem=dma((6,)),
         spare_sem=dma((1,)),
-        note_send=dma((2, others)), note_recv=dma((2, owners)),
-        tn_send=dma((peers,)), tn_recv=dma((tiles,)),
-        f_up=dma((owners,)), f_down=dma((owners,)), f_side=dma((beside, owners)), f_recv=dma((owners,)),
-        c_up=dma((owners,)), c_down=dma((owners,)), c_recv=dma((owners,)),
+        note_send=dma((2,)), note_recv=dma((2,)),
+        tn_send=dma((1,)), tn_recv=dma((1,)),
+        f_up=dma((deep,)), f_down=dma((deep,)), f_side=dma((beside, deep)), f_recv=dma((owners,)),
+        c_up=dma((deep,)), c_down=dma((deep,)), c_recv=dma((deep,)),
         cp_send=dma((beside, deep)), cp_recv=dma((owners,)),
         near_send=dma((2, owners)), far_send=dma((far, owners)),
         pass_send=dma((far, cores, mates, owners)), ft_recv=dma((owners, tiles)),
         above_send=dma((owners,)), above_recv=dma((owners,)),
         below_send=dma((owners,)), below_recv=dma((owners,)),
-        g_send=dma((peers, owners)), g_recv=dma((owners, tiles)),
-        gate_send=dma((owners,)), gate_recv=dma((owners,)),
+        g_send=dma((owners,)), g_recv=dma((owners,)),
+        gate_send=dma((1,)), gate_recv=dma((1,)),
         sb_send=dma((beside, deep)), sb_recv=dma((beside, deep)),
         sa_send=dma((beside, deep)), sa_recv=dma((beside, deep)),
-        fo_send=dma((deep,)), fi_recv=dma((deep,)),
+        fo_send=dma((2, deep)), fi_recv=dma((2, deep)),
     )
     held = 2 * frames.size * 4 * 2 + experts * taps * share * channels * 4 + owners * 8 * 128 * 4
     for ref in scratch.values():
@@ -698,8 +718,38 @@
             collective_id=0, has_side_effects=True, vmem_limit_bytes=held + (8 << 20)
         ),
         name="layer",
-    )(*(pltpu.with_memory_space_constraint(v, pltpu.HBM) for v in (frames, cot)), note, weight,
-      pltpu.with_memory_space_constraint(kernels, pltpu.HBM))
+    )(
+        pltpu.with_memory_space_constraint(frames, pltpu.HBM),
+        pltpu.with_memory_space_constraint(cot, pltpu.HBM),
+        note,
+        weight,
+        pltpu.with_memory_space_constraint(kernels, pltpu.HBM),
+    )
+
+
+def settle_kernel(count, *refs):
+    sems = refs[2 * count]
+    copies = [
+        pltpu.make_async_copy(refs[i], refs[count + i], sems.at[i]) for i in range(count)
+    ]
+    for copy in copies:
+        copy.start()
+    for copy in copies:
+        copy.wait()
+
+
+def settled(*arrays):
+    count = len(arrays)
+    anywhere = pl.BlockSpec(memory_space=pl.ANY)
+    return pl.pallas_call(
+        functools.partial(settle_kernel, count),
+        out_shape=[jax.ShapeDtypeStruct(a.shape, a.dtype) for a in arrays],
+        in_specs=[anywhere] * count,
+        out_specs=[pl.BlockSpec(memory_space=pltpu.HBM)] * count,
+        scratch_shapes=[pltpu.SemaphoreType.DMA((count,))],
+        compiler_params=pltpu.CompilerParams(vmem_limit_bytes=1 << 20),
+        name="settled",
+    )(*arrays)
 
 
 def shards(frames, kernels, experts, counts, gate_weights, cotangent):
@@ -728,6 +778,7 @@
     result, input_grad, gated, kernel_part = layer(
         frames[:, 0], cotangent[:, 0], note, weight, kernels, owners, tiles
     )
+    result, input_grad, kernel_part = settled(result, input_grad, kernel_part)
     kernel_part = jnp.swapaxes(kernel_part, 2, 3)
     gated = gated[:, :CAP, 0]
     selected = jnp.sum(jnp.where(slot_map, gated[:, :, None], 0.0), axis=1)

time: 77.5 us -> 68.7 us (0.89)
  Pallas kernels: 70.1 us -> 64.4 us
  local copies, waits for them, and re-layouts: 2.99 us -> 0.28 us
    pallas_call x1, Pallas kernels: 70.1 us -> 62.8 us  [layer(): pl.pallas_call(functools.partial(layer_kernel, deep, across, high, cores,...]
    unnamed x3 -> x0, local copies, waits for them, and re-layouts: 2.71 us -> none
    pallas_call x0 -> x1, Pallas kernels: none -> 1.52 us  [settled(): pl.pallas_call(functools.partial(settle_kernel, count), out_shape=[jax.Sh...]
where the time goes in v3:
time: 68.7 us; the launch traced here: 68.5 us
  Pallas kernels  64.4 us (94%)
  other arithmetic  3.17 us (5%)
    pallas_call x1, Pallas kernels, layer(): pl.pallas_call(functools.partial(layer_kernel, deep, across, high, cores,...  62.8 us
    pallas_call x1, Pallas kernels, settled(): pl.pallas_call(functools.partial(settle_kernel, count), out_shape=[jax.Sh...  1.52 us

profile of v3, /device:TPU:0, one launch (start us, length us, event | category | flops | bytes accessed | tf_op | source)
XLA Modules:
  0.0 68.5 jit_solution(18285200011048374224)
XLA Ops:
  0.6 0.7 %iota_compare_fusion.2 = pred[4,4]{1,0:T(4,128)(4,1)S(1)} fusion(s32[4]{0:T(128)} %bitcast.39), kind=kLoop, calls=%fused_computation.17 | loop fusion | flops 16 | bytes 32 | tf_op jit(solution)/shard_map/lt | solution.py:761
  1.4 0.7 %add_select_fusion = (s32[4,4]{1,0:T(4,128)S(1)}, s32[4,4]{1,0:T(4,128)S(1)}) fusion(s32[4,4]{1,0:T(4,128)} %bitcast.32), kind=kLoop, calls=%fused_computation.10 | loop fusion | flops 304 | bytes 192 | tf_op jit(solution)/shard_map/jit(remainder)/select_n | solution.py:769
  2.1 0.8 %select_reduce_fusion.1 = (f32[4,8]{1,0:T(4,128)S(1)}, pred[4,4,8]{2,1,0:T(4,128)(4,1)S(1)}) fusion(f32[4,4]{1,0:T(4,128)} %bitcast.33, pred[4,4]{1,0:T(4,128)(4,1)S(1)} %iota_compare_fusion.2, s32[4,4]{1,0:T(4,128)S(1)} %get-tuple-element.31), kind=kLoop, calls=%fused_computation.1 | loop fusion | flops 480 | bytes 400 | tf_op jit(solution)/shard_map/reduce_sum | solution.py:770
  2.8 0.1 select_reduce_fusion.2
  3.0 0.1 select_reduce_fusion.5
  3.1 0.1 copy.19
  3.2 0.1 copy.20
  3.3 62.8 %layer.1 = (bf16[4,64,256]{2,1,0:T(8,128)(2,1)S(1)}, bf16[4,64,256]{2,1,0:T(8,128)(2,1)S(1)}, f32[8,8,128]{2,1,0:T(8,128)S(1)}, f32[4,9,64,256]{3,2,1,0:T(8,128)S(1)}) custom-call(bf16[4,64,256]{2,1,0:T(8,128)(2,1)} %bitcast.25, bf16[4,64,256]{2,1,0:T(8,128)(2,1)} %bitcast.26, s32[8,1,128]{2,1,0:T(1,128)S(1)} %pad.8.note_ref, ...), custom_call_target="tpu_custom_call" | custom-call | tf_op jit(solution)/shard_map/layer/pallas_call | solution.py:706
  66.2 1.5 %settled.1 = (bf16[4,64,256]{2,1,0:T(8,128)(2,1)}, bf16[4,64,256]{2,1,0:T(8,128)(2,1)}, f32[4,9,64,256]{3,2,1,0:T(8,128)}) custom-call(bf16[4,64,256]{2,1,0:T(8,128)(2,1)S(1)} %get-tuple-element.11.refs_0_, bf16[4,64,256]{2,1,0:T(8,128)(2,1)S(1)} %get-tuple-element.12.refs_1_, f32[4,9,64,256]{3,2,1,0:T(8,128)S(1)} %get-tuple-element.13.refs_2_), custom_call_target="tpu_custom_call" | custom-call | tf_op jit(solution)/shard_map/settled/pallas_call | solution.py:744
  67.7 0.1 copy.21
  67.8 0.7 select_reduce_fusion
  (12 shorter events, 0.2 us)

commit v4 on v3

--- a/solution.py
+++ b/solution.py
@@ -42,8 +42,8 @@
 
 def layer_kernel(
     deep, across, high, cores, names,
-    frames_hbm, cot_hbm, note_ref, weight_ref, bank_hbm,
-    result_ref, input_ref, gated_ref, grad_ref, *rest,
+    frames_hbm, cot_hbm, ids_hbm, counts_hbm, gates_hbm, bank_hbm,
+    result_ref, input_ref, gate_ref, grad_ref, *rest,
 ):
     v = SimpleNamespace(**dict(zip(names, rest)))
     me, t = lax.axis_index("dp"), lax.axis_index("tile")
@@ -59,13 +59,18 @@
     bf16, f32 = jnp.bfloat16, jnp.float32
 
     load_bank = pltpu.make_async_copy(bank_hbm, v.bank, v.local_sem.at[0])
+    lists = [
+        pltpu.make_async_copy(ids_hbm, v.ids, v.local_sem.at[1]),
+        pltpu.make_async_copy(counts_hbm, v.counts, v.local_sem.at[2]),
+        pltpu.make_async_copy(gates_hbm, v.gates, v.local_sem.at[4]),
+    ]
+    for copy in lists:
+        copy.start()
     own_rows = pltpu.make_async_copy(frames_hbm, v.f.at[me, t], v.local_sem.at[3])
     own_rows.start()
     own_cot = pltpu.make_async_copy(cot_hbm, v.c.at[me], v.local_sem.at[5])
     own_cot.start()
     load_bank.start()
-    own_scalars = pltpu.make_async_copy(note_ref, v.os, v.local_sem.at[4])
-    own_scalars.start()
 
     barrier = pltpu.get_barrier_semaphore()
     for j in range(1, owners):
@@ -76,6 +81,43 @@
         pl.semaphore_signal(
             barrier, device_id=(me, lax.rem(t + j, tiles)), device_id_type=pl.DeviceIdType.MESH
         )
+
+    for copy in lists:
+        copy.wait()
+    slots = v.ids.shape[2]
+    lanes = lax.broadcasted_iota(jnp.int32, (1, 128), 1)
+
+    def owner_at(f, j):
+        return jnp.where(j < v.counts[0, f], lax.div(v.ids[f, 0, j], experts), -1)
+
+    wanted = jnp.zeros((1, 128), jnp.int32)
+    listed = jnp.zeros((1, 128), jnp.int32)
+    spot = [jnp.full((1, 128), -1, jnp.int32) for _ in range(cap)]
+    share_of = [jnp.zeros((1, 128), f32) for _ in range(cap)]
+    for f in range(frames):
+        hit = jnp.zeros((1, 128), jnp.int32)
+        gate = jnp.zeros((1, 128), f32)
+        for j in range(slots):
+            here = lanes == owner_at(f, j)
+            hit = jnp.where(here, 1, hit)
+            gate = jnp.where(here, v.gates[f, 0, j], gate)
+            wanted = jnp.where(here, lax.rem(v.ids[f, 0, j], experts), wanted)
+        for c in range(cap):
+            taken = jnp.logical_and(hit == 1, listed == c)
+            spot[c] = jnp.where(taken, f, spot[c])
+            share_of[c] = jnp.where(taken, gate, share_of[c])
+        listed = listed + hit
+    asked = jnp.concatenate(
+        [wanted] + spot + [jnp.zeros((127 - cap, 128), jnp.int32)], axis=0
+    )
+    shares = jnp.concatenate(share_of + [jnp.zeros((128 - cap, 128), f32)], axis=0)
+    asked, shares = jnp.transpose(asked), jnp.transpose(shares)
+    for o in range(owners):
+        v.note[o] = asked[o : o + 1]
+        v.weight[o] = shares[o : o + 1]
+    own_scalars = pltpu.make_async_copy(v.note, v.os, v.local_sem.at[4])
+    own_scalars.start()
+
     pl.semaphore_wait(barrier, owners - 1 + tiles - 1)
 
     def along(act, s, zs, fr, co):
@@ -213,7 +255,7 @@
             go(remote(v.go.at[s, tt], v.gi.at[s, t], v.g_send.at[s], v.g_recv.at[s], me, tt))
 
     def gates(s):
-        go(remote(v.gate.at[s], gated_ref.at[me], v.gate_send.at[0], v.gate_recv.at[0], s, t))
+        go(remote(v.gate.at[s], v.gated.at[me], v.gate_send.at[0], v.gate_recv.at[0], s, t))
 
     def side_act(act, s, zs, xj):
         act(
@@ -252,23 +294,23 @@
             peer = lax.rem(me + j, owners)
             go(
                 remote(
-                    note_ref.at[pl.ds(lax.div(peer, across) * across, across)], v.n.at[me],
+                    v.note.at[pl.ds(lax.div(peer, across) * across, across)], v.n.at[me],
                     v.note_send.at[0], v.note_recv.at[0], peer, t,
                 )
             )
             go(
                 remote(
-                    weight_ref.at[peer], v.w.at[me],
+                    v.weight.at[peer], v.w.at[me],
                     v.note_send.at[1], v.note_recv.at[1], peer, t,
                 )
             )
 
     send_notes()
     own_notes = pltpu.make_async_copy(
-        note_ref.at[pl.ds(z * across, across)], v.n.at[me], v.local_sem.at[1]
+        v.note.at[pl.ds(z * across, across)], v.n.at[me], v.local_sem.at[1]
     )
     own_notes.start()
-    own_weights = pltpu.make_async_copy(weight_ref.at[me], v.w.at[me], v.local_sem.at[2])
+    own_weights = pltpu.make_async_copy(v.weight.at[me], v.w.at[me], v.local_sem.at[2])
     own_weights.start()
     own_rows.wait()
     along(go, me, z, v.f.at[me, t], None)
@@ -441,7 +483,7 @@
 
         @pl.when(s == me)
         def _():
-            gated_ref[me] = sums
+            v.gated[me] = sums
 
         grad = (upstream * weight * slope).astype(bf16)
         turned = jnp.transpose(grad.astype(f32)).astype(bf16)
@@ -567,13 +609,15 @@
             ]
             for db in range(3):
                 for k in range(experts):
-                    v.gt[db, k * share : (k + 1) * share, span] = jnp.where(
+                    first = (db * experts + k) * share
+                    v.gt[first : first + share, span] = jnp.where(
                         e == k, moved[db], jnp.zeros_like(moved[db])
                     )
         for da in range(3):
+            term = jnp.dot(v.gt[...], v.xw[da], preferred_element_type=f32)
+            term = term.reshape(3, experts, share, channels)
             for db in range(3):
-                term = jnp.dot(v.gt[db], v.xw[da], preferred_element_type=f32)
-                grad_ref[:, 3 * da + db] += term.reshape(experts, share, channels)
+                grad_ref[:, 3 * da + db] += term[db]
 
     @pl.loop(0, count + (4 * step + 2))
     def _(n):
@@ -592,8 +636,18 @@
         stage(n - 2, weigh)
 
     some = pl.ds(0, owners - 1)
-    received(gated_ref.at[some], v.gate_recv.at[0])
+    received(v.gated.at[some], v.gate_recv.at[0])
     sent(v.gate.at[some], v.gate_send.at[0])
+    for f in range(frames):
+        at = jnp.full((1, 128), -1, jnp.int32)
+        for j in range(slots):
+            at = jnp.where(lanes == j, owner_at(f, j), at)
+        found = jnp.zeros((1, 128), f32)
+        for o in range(owners):
+            for c in range(cap):
+                owner = jnp.where(v.os[o, 0, 1 + c] == f, o, -2)
+                found = jnp.where(at == owner, v.gated[o, c : c + 1], found)
+        gate_ref[f] = found[:, :slots]
     sent(v.n.at[some], v.note_send.at[0])
     sent(v.w.at[some], v.note_send.at[1])
     sent(v.tn.at[pl.ds(0, tiles - 1)], v.tn_send.at[0])
@@ -639,7 +693,7 @@
         result_ref[f] = second.astype(bf16)
 
 
-def layer(frames, cot, note, weight, kernels, owners, tiles):
+def layer(frames, cot, ids, counts, gates, kernels, owners, tiles):
     deep, across = grid_of(owners)
     cores = 1 if tiles % 2 else 2
     high = tiles // cores
@@ -673,6 +727,12 @@
         go=pltpu.VMEM((owners, tiles, share, rows), bf16),
         gi=pltpu.VMEM((owners, tiles, share, rows), bf16),
         gate=pltpu.VMEM((owners, 8, 128), f32),
+        gated=pltpu.VMEM((owners, 8, 128), f32),
+        ids=pltpu.SMEM(ids.shape, i32),
+        counts=pltpu.SMEM(counts.shape, i32),
+        gates=pltpu.SMEM(gates.shape, f32),
+        note=pltpu.VMEM((owners, 1, 128), i32),
+        weight=pltpu.VMEM((owners, 1, 128), f32),
         sbo=pltpu.VMEM((beside, deep, count, columns, channels), bf16),
         sbi=pltpu.VMEM((beside, deep, count, columns, channels), bf16),
         sai=pltpu.VMEM((beside, deep, cap, columns, channels), bf16),
@@ -681,7 +741,7 @@
         total=pltpu.VMEM((2, count, columns, channels), f32),
         base=pltpu.VMEM((2, count, columns, channels), f32),
         xw=pltpu.VMEM((3, tiles * rows, channels), bf16),
-        gt=pltpu.VMEM((3, experts * share, tiles * rows), bf16),
+        gt=pltpu.VMEM((3 * experts * share, tiles * rows), bf16),
         local_sem=dma((6,)),
         spare_sem=dma((1,)),
         note_send=dma((2,)), note_recv=dma((2,)),
@@ -708,10 +768,10 @@
         out_shape=[
             jax.ShapeDtypeStruct(frames.shape, bf16),
             jax.ShapeDtypeStruct(frames.shape, bf16),
-            jax.ShapeDtypeStruct((owners, 8, 128), f32),
+            jax.ShapeDtypeStruct(gates.shape, f32),
             jax.ShapeDtypeStruct((experts, taps, share, channels), f32),
         ],
-        in_specs=[hbm, hbm, vmem, vmem, hbm],
+        in_specs=[hbm] * 6,
         out_specs=[vmem] * 4,
         scratch_shapes=list(scratch.values()),
         compiler_params=pltpu.CompilerParams(
@@ -719,11 +779,10 @@
         ),
         name="layer",
     )(
-        pltpu.with_memory_space_constraint(frames, pltpu.HBM),
-        pltpu.with_memory_space_constraint(cot, pltpu.HBM),
-        note,
-        weight,
-        pltpu.with_memory_space_constraint(kernels, pltpu.HBM),
+        *(
+            pltpu.with_memory_space_constraint(value, pltpu.HBM)
+            for value in (frames, cot, ids, counts, gates, kernels)
+        )
     )
 
 
@@ -755,35 +814,13 @@
 def shards(frames, kernels, experts, counts, gate_weights, cotangent):
     owners = lax.axis_size("dp")
     tiles = lax.axis_size("tile")
-    local = kernels.shape[0]
-    chosen = experts[:, 0]
-    frame_count, slots = chosen.shape
-    active = jnp.arange(slots)[None, :] < counts[:, 0][:, None]
-    owner_of = chosen // local
-    hit = (owner_of[:, :, None] == jnp.arange(owners)) & active[:, :, None]
-    wanted = jnp.any(hit, axis=1)
-    position = jnp.cumsum(wanted.astype(jnp.int32), axis=0) - 1
-    slot_map = wanted.T[:, None, :] & (
-        position.T[:, None, :] == jnp.arange(CAP)[None, :, None]
+    result, input_grad, gate_grad, kernel_part = settled(
+        *layer(
+            frames[:, 0], cotangent[:, 0], experts, counts.T, gate_weights, kernels, owners, tiles
+        )
     )
-    request = jnp.max(jnp.where(hit, (chosen % local)[:, :, None], 0), axis=(0, 1))
-    tile_gate = jnp.sum(jnp.where(hit, gate_weights[:, 0][:, :, None], 0.0), axis=1)
-    weight = jnp.sum(jnp.where(slot_map, tile_gate.T[:, None, :], 0.0), axis=2)
-    place = jnp.sum(
-        jnp.where(slot_map, jnp.arange(1, frame_count + 1)[None, None, :], 0), axis=2
-    ) - 1
-    note = jnp.concatenate([request[:, None], place], axis=1).astype(jnp.int32)
-    note = jnp.pad(note[:, None, :], ((0, 0), (0, 0), (0, 128 - note.shape[1])))
-    weight = jnp.pad(weight[:, None, :], ((0, 0), (0, 0), (0, 128 - CAP)))
-    result, input_grad, gated, kernel_part = layer(
-        frames[:, 0], cotangent[:, 0], note, weight, kernels, owners, tiles
-    )
-    result, input_grad, kernel_part = settled(result, input_grad, kernel_part)
     kernel_part = jnp.swapaxes(kernel_part, 2, 3)
-    gated = gated[:, :CAP, 0]
-    selected = jnp.sum(jnp.where(slot_map, gated[:, :, None], 0.0), axis=1)
-    gate_grad = jnp.sum(jnp.where(hit, selected.T[:, None, :], 0.0), axis=2)
-    return (result[:, None], input_grad[:, None], gate_grad[:, None, :], kernel_part)
+    return (result[:, None], input_grad[:, None], gate_grad, kernel_part)
 
 
 def solution(mesh):

time: 68.7 us -> 65 us (0.946)
  other arithmetic: 3.17 us -> 0 us
    reduce_sum x5 -> x0, other arithmetic: 1.56 us -> none  [the longest x1 0.77 us: shards(): jnp.sum(jnp.where(hit, gate_weights[:, 0][:, :, None], 0.0), axis=1)]
    lt x1 -> x0, other arithmetic: 0.73 us -> none  [shards(): active = jnp.arange(slots)[None, :] < counts[:, 0][:, None]]
    select_n x1 -> x0, other arithmetic: 0.69 us -> none  [shards(): chosen % local]
where the time goes in v4:
time: 65 us; the launch traced here: 64.9 us
  Pallas kernels  64.2 us (99%)
    pallas_call x1, Pallas kernels, layer(): pl.pallas_call(functools.partial(layer_kernel, deep, across, high, cores,...  62.7 us
    pallas_call x1, Pallas kernels, settled(): pl.pallas_call(functools.partial(settle_kernel, count), out_shape=[jax.Sh...  1.53 us

profile of v4, /device:TPU:0, one launch (start us, length us, event | category | flops | bytes accessed | tf_op | source)
XLA Modules:
  0.0 64.9 jit_solution(530062139243243849)
XLA Ops:
  0.6 62.7 %layer.1 = (bf16[4,64,256]{2,1,0:T(8,128)(2,1)S(1)}, bf16[4,64,256]{2,1,0:T(8,128)(2,1)S(1)}, f32[4,1,4]{2,1,0:T(1,128)S(1)}, f32[4,9,64,256]{3,2,1,0:T(8,128)S(1)}) custom-call(bf16[4,64,256]{2,1,0:T(8,128)(2,1)} %bitcast.10, bf16[4,64,256]{2,1,0:T(8,128)(2,1)} %bitcast.11, s32[4,1,4]{2,1,0:T(1,128)} %ids_hbm.1, s32[1,4]{1,0:T(1,128)} %bitcast.12, ...), custom_call_target="tpu_custom_call" | custom-call | tf_op jit(solution)/shard_map/layer/pallas_call | solution.py:766
  63.3 1.5 %settled.1 = (bf16[4,64,256]{2,1,0:T(8,128)(2,1)}, bf16[4,64,256]{2,1,0:T(8,128)(2,1)}, f32[4,1,4]{2,1,0:T(1,128)}, f32[4,9,64,256]{3,2,1,0:T(8,128)}) custom-call(bf16[4,64,256]{2,1,0:T(8,128)(2,1)S(1)} %get-tuple-element.12.refs_0_, bf16[4,64,256]{2,1,0:T(8,128)(2,1)S(1)} %get-tuple-element.13.refs_1_, f32[4,1,4]{2,1,0:T(1,128)S(1)} %get-tuple-element.14.refs_2_, ...), custom_call_target="tpu_custom_call" | custom-call | tf_op jit(solution)/shard_map/settled/pallas_call | solution.py:803

commit v5 on v4

--- a/solution.py
+++ b/solution.py
@@ -619,15 +619,15 @@
             for db in range(3):
                 grad_ref[:, 3 * da + db] += term[db]
 
-    @pl.loop(0, count + (4 * step + 2))
+    @pl.loop(0, count + count)
     def _(n):
         pl.when(n == step)(load_bank.wait)
         pl.when(n == (step + 3))(settle)
         stage(n - step, compute)
         stage(n - (step + 3), to_side, lead=False)
         stage(n - 4 * step, far_act, lead=True)
-        stage(n - (4 * step + 2), far_back, lead=True)
-        stage(n - (4 * step + 2), lambda s, zs, xj: far_rows(go, s))
+        stage(n - count, far_back, lead=True)
+        stage(n - count, lambda s, zs, xj: far_rows(go, s))
         pl.when(n > 1)(lambda: stage(n, arrive))
 
     @pl.loop(0, count + 2)

time: 65 us -> 63.7 us (0.980)
  Pallas kernels: 64.2 us -> 62.9 us
    pallas_call x1, Pallas kernels: 62.7 us -> 61.3 us  [layer(): pl.pallas_call(functools.partial(layer_kernel, deep, across, high, cores,...]
where the time goes in v5:
time: 63.7 us; the launch traced here: 63.5 us
  Pallas kernels  62.9 us (99%)
  between operations  0.64 us (1%)
    pallas_call x1, Pallas kernels, layer(): pl.pallas_call(functools.partial(layer_kernel, deep, across, high, cores,...  61.3 us
    pallas_call x1, Pallas kernels, settled(): pl.pallas_call(functools.partial(settle_kernel, count), out_shape=[jax.Sh...  1.53 us

profile of v5, /device:TPU:0, one launch (start us, length us, event | category | flops | bytes accessed | tf_op | source)
XLA Modules:
  0.0 63.5 jit_solution(11761650375568976782)
XLA Ops:
  0.6 61.3 %layer.1 = (bf16[4,64,256]{2,1,0:T(8,128)(2,1)S(1)}, bf16[4,64,256]{2,1,0:T(8,128)(2,1)S(1)}, f32[4,1,4]{2,1,0:T(1,128)S(1)}, f32[4,9,64,256]{3,2,1,0:T(8,128)S(1)}) custom-call(bf16[4,64,256]{2,1,0:T(8,128)(2,1)} %bitcast.10, bf16[4,64,256]{2,1,0:T(8,128)(2,1)} %bitcast.11, s32[4,1,4]{2,1,0:T(1,128)} %ids_hbm.1, s32[1,4]{1,0:T(1,128)} %bitcast.12, ...), custom_call_target="tpu_custom_call" | custom-call | tf_op jit(solution)/shard_map/layer/pallas_call | solution.py:766
  62.0 1.5 %settled.1 = (bf16[4,64,256]{2,1,0:T(8,128)(2,1)}, bf16[4,64,256]{2,1,0:T(8,128)(2,1)}, f32[4,1,4]{2,1,0:T(1,128)}, f32[4,9,64,256]{3,2,1,0:T(8,128)}) custom-call(bf16[4,64,256]{2,1,0:T(8,128)(2,1)S(1)} %get-tuple-element.12.refs_0_, bf16[4,64,256]{2,1,0:T(8,128)(2,1)S(1)} %get-tuple-element.13.refs_1_, f32[4,1,4]{2,1,0:T(1,128)S(1)} %get-tuple-element.14.refs_2_, ...), custom_call_target="tpu_custom_call" | custom-call | tf_op jit(solution)/shard_map/settled/pallas_call | solution.py:803

commit v6 on v5

--- a/solution.py
+++ b/solution.py
@@ -55,7 +55,7 @@
     cap = CAP
     rows = cap * columns
     has_above, has_below = t > 0, t < tiles - 1
-    t_above, t_below = lax.rem(t + tiles - 1, tiles), lax.rem(t + 1, tiles)
+    t_above, t_below = t - has_above.astype(jnp.int32), t + has_below.astype(jnp.int32)
     bf16, f32 = jnp.bfloat16, jnp.float32
 
     load_bank = pltpu.make_async_copy(bank_hbm, v.bank, v.local_sem.at[0])

time: 63.7 us -> 63.7 us (level)
  no operation moved by 1% of the time
where the time goes in v6:
time: 63.7 us; the launch traced here: 63.5 us
  Pallas kernels  62.9 us (99%)
  between operations  0.64 us (1%)
    pallas_call x1, Pallas kernels, layer(): pl.pallas_call(functools.partial(layer_kernel, deep, across, high, cores,...  61.4 us
    pallas_call x1, Pallas kernels, settled(): pl.pallas_call(functools.partial(settle_kernel, count), out_shape=[jax.Sh...  1.53 us

profile of v6, /device:TPU:0, one launch (start us, length us, event | category | flops | bytes accessed | tf_op | source)
XLA Modules:
  0.0 63.5 jit_solution(5227005052126531633)
XLA Ops:
  0.6 61.4 %layer.1 = (bf16[4,64,256]{2,1,0:T(8,128)(2,1)S(1)}, bf16[4,64,256]{2,1,0:T(8,128)(2,1)S(1)}, f32[4,1,4]{2,1,0:T(1,128)S(1)}, f32[4,9,64,256]{3,2,1,0:T(8,128)S(1)}) custom-call(bf16[4,64,256]{2,1,0:T(8,128)(2,1)} %bitcast.10, bf16[4,64,256]{2,1,0:T(8,128)(2,1)} %bitcast.11, s32[4,1,4]{2,1,0:T(1,128)} %ids_hbm.1, s32[1,4]{1,0:T(1,128)} %bitcast.12, ...), custom_call_target="tpu_custom_call" | custom-call | tf_op jit(solution)/shard_map/layer/pallas_call | solution.py:766
  62.0 1.5 %settled.1 = (bf16[4,64,256]{2,1,0:T(8,128)(2,1)}, bf16[4,64,256]{2,1,0:T(8,128)(2,1)}, f32[4,1,4]{2,1,0:T(1,128)}, f32[4,9,64,256]{3,2,1,0:T(8,128)}) custom-call(bf16[4,64,256]{2,1,0:T(8,128)(2,1)S(1)} %get-tuple-element.12.refs_0_, bf16[4,64,256]{2,1,0:T(8,128)(2,1)S(1)} %get-tuple-element.13.refs_1_, f32[4,1,4]{2,1,0:T(1,128)S(1)} %get-tuple-element.14.refs_2_, ...), custom_call_target="tpu_custom_call" | custom-call | tf_op jit(solution)/shard_map/settled/pallas_call | solution.py:803
